TPU v7x, 512 devices: a whole 4x4x16 slice. The times are simulated.
512 devices in a mesh: grp: 16 (over z), shard: 32 (over y, x, core).
Axes of the slice: x: 4, y: 4, z: 16, core: 2. Of those that a mesh axis runs over, the one named last changes fastest.
Arguments:
- activations: bfloat16 [1024, 5120], P('grp', 'shard'), may hold values from -6 to 6
- grad_outputs: bfloat16 [1024, 27648], P('shard', 'grp'), may hold values from -6 to 6
- basis_in: bfloat16 [5120, 2560], P('shard', 'grp'), may hold values from -0.078125 to 0.078125
- basis_out: bfloat16 [27648, 13824], P('grp', 'shard'), may hold values from -0.0390625 to 0.0390625
- query_grads: bfloat16 [16, 2560, 13824], P('grp', None, 'shard'), may hold values from -0.0009765625 to 0.0009765625
Outputs:
- scores: float32 [16, 1024], P('grp', 'shard')
All inputs are finite; a program needn't handle non-finite values.
Results may differ from a plain program's by a relative error of at most 0.0041.
Values may be sent and summed in bfloat16 or wider, within the bound.
No kernel may reach another device: no remote copies, remote signals or barrier semaphores. Data moves between devices by JAX's collectives and lax.ppermute only.
A program may use at most 64 MiB of HBM per device.

v0:
```python
import jax
import jax.numpy as jnp
from jax import lax
from jax.sharding import PartitionSpec as P


def local(activations, grad_outputs, basis_in, basis_out, query_grads):
    full_in = lax.all_gather(basis_in, "grp", axis=1, tiled=True)
    act_terms = lax.dot_general(
        full_in, activations, (((0,), (1,)), ((), ())), preferred_element_type=jnp.float32
    )
    act_local = lax.psum(act_terms, "shard").astype(jnp.bfloat16)
    act_rot = lax.all_gather(act_local, "grp", axis=1, tiled=True)
    out_terms = jnp.dot(
        lax.all_gather(grad_outputs, "shard", axis=0, tiled=True),
        basis_out,
        preferred_element_type=jnp.float32,
    )
    out_rot = lax.psum(out_terms, "grp").astype(jnp.bfloat16)
    mixed = lax.dot_general(
        act_rot, query_grads[0], (((0,), (0,)), ((), ())), preferred_element_type=jnp.float32
    )
    partial_scores = jnp.sum(mixed * out_rot.astype(jnp.float32), axis=1)
    return lax.psum_scatter(partial_scores[None, :], "shard", scatter_dimension=1, tiled=True)


def solution(mesh):
    placed = (
        P("grp", "shard"),
        P("shard", "grp"),
        P("shard", "grp"),
        P("grp", "shard"),
        P("grp", None, "shard"),
    )
    return jax.shard_map(
        local, mesh=mesh, in_specs=placed, out_specs=P("grp", "shard"), check_vma=False
    )
```

profile of v0, /device:TPU:2, one launch (start us, length us, event | category | flops | bytes accessed | tf_op | source)
XLA Modules:
  0.0 392.9 jit_solution(17154068372020771227)
XLA Ops:
  6.5 0.0 copy-start
  6.5 0.0 all-gather.5.cloned.1.call-start
  6.5 0.7 all-gather.5.cloned.1.call-update
  7.3 0.0 all-gather.3.cloned.1.call-start
  7.3 1.0 copy.6
  8.3 43.3 %all_gather.9 = bf16[160,2560]{0,1:T(8,128)(2,1)S(1)} all-gather(bf16[160,160]{0,1:T(8,128)(2,1)S(1)} %copy.6), channel_id=1, replica_groups=mesh['grp'=16,'shard'=32] {'grp'}, dimensions={1}, use_global_device_ids=true | all-gather | bytes 870400 | tf_op jit(solution)/shard_map/all_gather | solution.py:8
  51.6 1.3 fusion.4
  52.9 126.1 %all-reduce.3 = bf16[2560,64]{0,1:T(8,128)(2,1)} all-reduce(f32[2560,64]{0,1:T(8,128)S(1)} %fusion.4), channel_id=1, replica_groups=mesh['grp'=16,'shard'=32] {'shard'}, use_global_device_ids=true, to_apply=%region_0.0 | all-reduce | flops 163840 | bytes 983040 | tf_op jit(solution)/shard_map/psum | solution.py:12
  178.9 0.0 all-gather.3.cloned.1.call-update
  179.0 0.0 reduce-scatter.4.cloned.1.call-start
  179.0 0.0 all-gather.5.cloned.1.call-done
  179.0 5.5 %fusion.5 = f32[1024,432]{0,1:T(8,128)} fusion(bf16[1024,1728]{1,0:T(8,128)(2,1)} %all-gather.5.cloned.1.call-done, bf16[1728,432]{0,1:T(8,128)(2,1)} %param.8), kind=kOutput, calls=%fused_computation.4 | convolution fusion | flops 1528823808 | bytes 6801408 | tf_op jit(solution)/shard_map/dot_general | solution.py:14
  184.6 91.9 %all-reduce.2 = bf16[1024,432]{0,1:T(8,128)(2,1)S(1)} all-reduce(f32[1024,432]{0,1:T(8,128)} %fusion.5), channel_id=1, replica_groups=mesh['grp'=16,'shard'=32] {'grp'}, use_global_device_ids=true, to_apply=%region_1.0 | all-reduce | flops 442368 | bytes 2654208 | tf_op jit(solution)/shard_map/psum | solution.py:19
  276.4 4.1 %all-gather.3.cloned.1.call-done = bf16[2560,1024]{0,1:T(8,128)(2,1)} async-done(((bf16[2560,64]{0,1:T(8,128)(2,1)}), bf16[2560,1024]{0,1:T(8,128)(2,1)}) %all-gather.3.cloned.1.call-update) | async-done | bytes 5242896 | tf_op jit(solution)/shard_map/all_gather | solution.py:13
  280.5 0.0 copy-done
  280.5 5.0 %multiply_reduce_fusion = f32[1024]{0:T(1024)S(1)} fusion(bf16[2560,1024]{0,1:T(8,128)(2,1)} %all-gather.3.cloned.1.call-done, bf16[1,2560,432]{1,2,0:T(8,128)(2,1)S(1)} %copy-done, bf16[1024,432]{0,1:T(8,128)(2,1)S(1)} %all-reduce.2), kind=kOutput, calls=%fused_computation.2 | convolution fusion | flops 2266250240 | bytes 8343552 | tf_op jit(solution)/shard_map/dot_general | solution.py:20
  285.5 1.0 copy.7
  286.5 0.0 reduce-scatter.4.cloned.1.call-update
  286.5 98.5 %reduce-scatter.4.cloned.1.call-done = f32[32,1]{1,0:T(8,128)} async-done(((f32[1024,1]{1,0:T(8,128)}), f32[32,1]{1,0:T(8,128)}) %reduce-scatter.4.cloned.1.call-update) | async-done | bytes 144
  385.1 1.3 copy.8
Async XLA Ops:
  6.5 274.0 %copy-start = (bf16[1,2560,432]{1,2,0:T(8,128)(2,1)S(1)}, bf16[1,2560,432]{1,2,0:T(8,128)(2,1)}, u32[]{:S(2)}) copy-start(bf16[1,2560,432]{1,2,0:T(8,128)(2,1)} %param.9) | copy-start | bytes 6635524
  6.5 172.5 %all-gather.5.cloned.1.call-start = ((), (), s32[]{:S(2)}) async-start(), calls=%async_computation.2 | async-start | bytes 3784704 | tf_op jit(solution)/shard_map/all_gather | solution.py:15
  7.3 273.3 %all-gather.3.cloned.1.call-start = ((), (), s32[]{:S(2)}) async-start(), calls=%async_computation.1 | async-start | bytes 5570560 | tf_op jit(solution)/shard_map/all_gather | solution.py:13
  179.0 206.1 %reduce-scatter.4.cloned.1.call-start = ((), (), s32[]{:S(2)}) async-start(), calls=%async_computation.3 | async-start | bytes 540672
Sparse Core Ops, SparseCore 0:
  10.5 64.9 all-gather.4
  179.1 101.3 all-gather.2
  286.7 98.3 reduce-scatter.3
where the time goes:
time: 393 us
  blocking collectives  261 us (66%)
  waiting for transfers between devices  103 us (26%)
  between operations  13.1 us (3%)
  matrix products  11.8 us (3%)
    psum x1, blocking collectives, local(): act_local = lax.psum(act_terms, 'shard').astype(jnp.bfloat16)  126 us
    unnamed x4, waiting for transfers between devices  99.3 us
    psum x1, blocking collectives, local(): out_rot = lax.psum(out_terms, 'grp').astype(jnp.bfloat16)  91.9 us
    all_gather x1, blocking collectives, local(): full_in = lax.all_gather(basis_in, 'grp', axis=1, tiled=True)  43.3 us
  transfers between devices with their start and end apart: 3, of which 2 were waited for; matrix products, arithmetic and copies ran while one was open for 2% of the time, Pallas kernels for 0%

commit v1 on v0

v1 whole, which is shorter than its diff:
```python
import jax
import jax.numpy as jnp
from jax import lax
from jax.sharding import PartitionSpec as P


F32 = jnp.float32
BF16 = jnp.bfloat16
NT = (((1,), (1,)), ((), ()))


def product(left, right):
    return lax.dot_general(left, right, NT, preferred_element_type=F32)


def spread(block, axis, count, groups):
    copies = jnp.broadcast_to(block[None], (count, *block.shape))
    return lax.all_to_all(copies, axis, 0, 0, axis_index_groups=groups)


def local(activations, grad_outputs, basis_in, basis_out, query_grads):
    n_grp = lax.axis_size("grp")
    n_shard = lax.axis_size("shard")
    chips = n_shard // 2
    one_core = [[2 * chip + core for chip in range(chips)] for core in range(2)]
    other_core = [(at, at ^ 1) for at in range(n_shard)]
    pairs = [(at, at ^ 1) for at in range(n_grp)]
    cross_pairs = [(at, (at + (1 if at % 2 else -1)) % n_grp) for at in range(n_grp)]
    alike = [list(range(parity, n_grp, 2)) for parity in range(2)]
    rows = grad_outputs.shape[0]
    half = chips * rows
    eig = basis_in.shape[1]
    parity = lax.axis_index("grp") % 2

    grads = spread(grad_outputs, "shard", chips, one_core)
    basis_own = basis_out.T
    basis_other = lax.ppermute(basis_own, "shard", other_core)
    query_own = query_grads[0].T
    query_other = lax.ppermute(query_own, "shard", other_core)
    acts = lax.all_gather(activations, "grp", axis=0, tiled=True)

    act_terms = jnp.dot(acts, basis_in, preferred_element_type=F32)
    act_terms = lax.all_to_all(act_terms.reshape(n_shard, rows, eig), "shard", 0, 0)
    act_own = jnp.sum(act_terms, axis=0).astype(BF16)

    grads = grads.reshape(n_grp // 2, 2, rows, -1)
    passed = lax.dynamic_index_in_dim(grads, 1 - parity, 1, keepdims=False).reshape(half // 2, -1)
    passed_own = product(passed, basis_own).astype(BF16)
    passed_other = product(passed, basis_other).astype(BF16)
    got_own = lax.ppermute(passed_own, "grp", pairs)
    got_other = lax.ppermute(passed_other, "grp", cross_pairs)
    kept = lax.dynamic_index_in_dim(grads, parity, 1, keepdims=False).reshape(half // 2, -1)
    kept_own = product(kept, basis_own) + got_own.astype(F32)
    kept_other = product(kept, basis_other) + got_other.astype(F32)
    out_terms = jnp.concatenate([kept_own, kept_other], axis=1).astype(BF16)
    out_terms = lax.all_to_all(
        out_terms.reshape(n_grp // 2, rows, -1), "grp", 0, 0, axis_index_groups=alike
    )
    out_own = jnp.sum(out_terms.astype(F32), axis=0).astype(BF16)

    act_cols = lax.all_gather(act_own, "grp", axis=0, tiled=False)
    act_rot = act_cols.transpose(1, 0, 2).reshape(rows, n_grp * eig)
    act_rot = spread(act_rot, "shard", chips, one_core).reshape(half, n_grp * eig)
    out_rot = lax.all_gather(out_own, "grp", axis=0, tiled=True)

    query = jnp.concatenate([query_own, query_other], axis=0)
    partial = jnp.sum(product(act_rot, query) * out_rot.astype(F32), axis=1)
    partial = jnp.broadcast_to(partial.reshape(chips, 1, rows), (chips, 8, rows))
    partial = lax.all_to_all(partial, "shard", 0, 0, axis_index_groups=one_core)
    return jnp.sum(partial[:, :1], axis=0)


def solution(mesh):
    placed = (
        P("grp", "shard"),
        P("shard", "grp"),
        P("shard", "grp"),
        P("grp", "shard"),
        P("grp", None, "shard"),
    )
    return jax.shard_map(
        local, mesh=mesh, in_specs=placed, out_specs=P("grp", "shard"), check_vma=False
    )
```

time: 393 us -> 200 us (0.51)
  blocking collectives: 261 us -> 130 us
  waiting for transfers between devices: 103 us -> 4.48 us
  starting transfers between devices: 0.08 us -> 39.9 us
  between operations: 13.1 us -> 0.21 us
    psum x2 -> x0, blocking collectives: 218 us -> none  [the longest x1 126 us: local(): act_local = lax.psum(act_terms, 'shard').astype(jnp.bfloat16)]
    unnamed x4 -> x0, waiting for transfers between devices: 99.3 us -> none
    all_gather x1 -> x3, blocking collectives: 43.3 us -> 117 us  [the longest x1 45.9 us: local(): act_cols = lax.all_gather(act_own, 'grp', axis=0, tiled=False)]
    all_to_all x0 -> x4, starting transfers between devices: none -> 31.4 us  [the longest x2 16.8 us: spread(): return lax.all_to_all(copies, axis, 0, 0, axis_index_groups=groups)]
    all_to_all x0 -> x1, blocking collectives: none -> 13.1 us  [local(): partial = lax.all_to_all(partial, 'shard', 0, 0, axis_index_groups=one_core)]
    ppermute x0 -> x4, starting transfers between devices: none -> 8.45 us  [the longest x1 2.71 us: local(): got_own = lax.ppermute(passed_own, 'grp', pairs)]
    broadcast_in_dim x0 -> x5, local copies, waits for them, and re-layouts: none -> 4.57 us  [the longest x3 4.48 us: spread(): copies = jnp.broadcast_to(block[None], (count, *block.shape))]
    ppermute x0 -> x4, waiting for transfers between devices: none -> 4.47 us  [the longest x1 3.9 us: local(): got_other = lax.ppermute(passed_other, 'grp', cross_pairs)]
  transfers between devices with their start and end apart: 3 -> 8, of which waited for: 2 -> 2; matrix products, arithmetic and copies ran while one was open for 2% -> 6% of each run, Pallas kernels for 0% -> 0%
where the time goes in v1:
time: 200 us; the launch traced here: 199 us
  blocking collectives  130 us (65%)
  starting transfers between devices  39.9 us (20%)
  matrix products  15.5 us (8%)
  local copies, waits for them, and re-layouts  6.33 us (3%)
  waiting for transfers between devices  4.48 us (2%)
  other arithmetic  2.27 us (1%)
    all_gather x1, blocking collectives, local(): act_cols = lax.all_gather(act_own, 'grp', axis=0, tiled=False)  45.9 us
    all_gather x1, blocking collectives, local(): acts = lax.all_gather(activations, 'grp', axis=0, tiled=True)  36.5 us
    all_gather x1, blocking collectives, local(): out_rot = lax.all_gather(out_own, 'grp', axis=0, tiled=True)  34.5 us
    all_to_all x2, starting transfers between devices, spread(): return lax.all_to_all(copies, axis, 0, 0, axis_index_groups=groups)  16.8 us
    dot_general x5, matrix products, product(): return lax.dot_general(left, right, NT, preferred_element_type=F32)  14.2 us
    all_to_all x1, blocking collectives, local(): partial = lax.all_to_all(partial, 'shard', 0, 0, axis_index_groups=one_core)  13.1 us
    all_to_all x1, starting transfers between devices, local(): lax.all_to_all(act_terms.reshape(n_shard, rows, eig), 'shard', 0, 0)  7.46 us
    all_to_all x1, starting transfers between devices, local(): lax.all_to_all(out_terms.reshape(n_grp // 2, rows, -1), 'grp', 0, 0, axis...  7.23 us
  transfers between devices with their start and end apart: 8, of which 2 were waited for; matrix products, arithmetic and copies ran while one was open for 6% of the time, Pallas kernels for 0%

profile of v1, /device:TPU:2, one launch (start us, length us, event | category | flops | bytes accessed | tf_op | source)
XLA Modules:
  0.0 198.7 jit_solution(15232957102977068931)
XLA Ops:
  0.0 0.0 copy-start
  0.0 2.4 %broadcast_in_dim.22 = bf16[16,32,1728]{2,1,0:T(8,128)(2,1)} broadcast(bf16[32,1728]{1,0:T(8,128)(2,1)} %param.6), dimensions={1,2} | broadcast | bytes 1880064 | tf_op jit(solution)/shard_map/broadcast_in_dim | solution.py:17
  2.4 0.0 copy-start.2
  2.4 9.5 %all-to-all-start.2 = ((bf16[16,32,1728]{2,1,0:T(8,128)(2,1)}), bf16[16,32,1728]{2,1,0:T(8,128)(2,1)S(1)}, u32[]{:S(2)}, u32[]{:S(2)}) async-start(bf16[16,32,1728]{2,1,0:T(8,128)(2,1)} %broadcast_in_dim.22), calls=%async_computation.2 | async-start | bytes 3670016 | tf_op jit(solution)/shard_map/all_to_all | solution.py:18
  11.9 1.9 collective-permute-start.2
  13.8 0.0 copy-done.2
  13.8 36.5 %all_gather.10 = bf16[1024,160]{1,0:T(8,128)(2,1)S(1)} all-gather(bf16[64,160]{1,0:T(8,128)(2,1)S(1)} %copy-done.2), channel_id=1, replica_groups=mesh['grp'=16,'shard'=32] {'grp'}, dimensions={0}, use_global_device_ids=true | all-gather | bytes 348160 | tf_op jit(solution)/shard_map/all_gather | solution.py:40
  50.4 0.0 copy-done
  50.4 1.3 fusion.8
  51.7 0.0 all-to-all-done.2
  51.7 7.5 %all-to-all-start = ((f32[32,32,160]{2,1,0:T(8,128)}), f32[32,32,160]{2,1,0:T(8,128)S(1)}, u32[]{:S(2)}, u32[]{:S(2)}) async-start(f32[32,32,160]{2,1,0:T(8,128)} %bitcast.28), calls=%async_computation | async-start | bytes 2097152 | tf_op jit(solution)/shard_map/all_to_all | solution.py:43
  59.1 0.1 constant_dynamic-slice_fusion
  59.3 0.0 copy-start.1
  59.3 0.0 collective-permute-done.2
  59.3 2.3 %convolution_convert_fusion = bf16[256,432]{0,1:T(8,128)(2,1)S(1)} fusion(bf16[256,1728]{1,0:T(8,128)(2,1)S(1)} %bitcast.34, bf16[432,1728]{1,0:T(8,128)(2,1)} %collective-permute-done.2), kind=kOutput, calls=%fused_computation.6 | convolution fusion | flops 382316544 | bytes 2598912 | tf_op jit(solution)/shard_map/dot_general | solution.py:13
  61.6 1.9 collective-permute-start.3
  63.6 2.0 %convolution_convert_fusion.1 = bf16[256,432]{0,1:T(8,128)(2,1)S(1)} fusion(bf16[256,1728]{1,0:T(8,128)(2,1)S(1)} %bitcast.35, bf16[1728,432]{0,1:T(8,128)(2,1)} %param.8), kind=kOutput, calls=%fused_computation.7 | convolution fusion | flops 382316544 | bytes 2598912 | tf_op jit(solution)/shard_map/dot_general | solution.py:13
  65.6 2.7 %collective-permute-start.1 = (bf16[256,432]{0,1:T(8,128)(2,1)S(1)}, bf16[256,432]{0,1:T(8,128)(2,1)S(1)}, u32[]{:S(2)}, u32[]{:S(2)}) collective-permute-start(bf16[256,432]{0,1:T(8,128)(2,1)S(1)} %convolution_convert_fusion.1), channel_id=1, source_target_pairs={{0,32},{32,0},{64,96},{96,64},{128,160},{160,128},{192,224},{224,1... | collective-permute-start | bytes 663560 | tf_op jit(solution)/shard_map/ppermute | solution.py:50
  68.3 3.9 %collective-permute-done.3 = bf16[256,432]{0,1:T(8,128)(2,1)S(1)} collective-permute-done((bf16[256,432]{0,1:T(8,128)(2,1)S(1)}, bf16[256,432]{0,1:T(8,128)(2,1)S(1)}, u32[]{:S(2)}, u32[]{:S(2)}) %collective-permute-start.3) | collective-permute-done | bytes 221216 | tf_op jit(solution)/shard_map/ppermute | solution.py:51
  72.2 0.0 copy-done.1
  72.2 2.0 %fusion.6 = bf16[256,432]{0,1:T(8,128)(2,1)S(1)} fusion(bf16[256,1728]{1,0:T(8,128)(2,1)S(1)} %bitcast.32, bf16[432,1728]{1,0:T(8,128)(2,1)} %collective-permute-done.2, bf16[256,432]{0,1:T(8,128)(2,1)S(1)} %collective-permute-done.3), kind=kOutput, calls=%fused_computation.8 | convolution fusion | flops 382537728 | bytes 2820096 | tf_op jit(solution)/shard_map/dot_general | solution.py:13
  74.2 0.1 copy.26
  74.3 0.6 collective-permute-done.1
  74.9 2.3 %add_convert_fusion = bf16[256,432]{0,1:T(8,128)(2,1)S(1)} fusion(bf16[256,432]{0,1:T(8,128)(2,1)S(1)} %collective-permute-done.1, bf16[256,1728]{1,0:T(8,128)(2,1)} %bitcast.33, bf16[1728,432]{0,1:T(8,128)(2,1)} %param.8), kind=kOutput, calls=%fused_computation.10 | convolution fusion | flops 382537728 | bytes 2820096 | tf_op jit(solution)/shard_map/dot_general | solution.py:13
  77.2 0.1 copy.25
  77.4 0.9 pad_maximum_fusion
  78.3 0.0 all-to-all-done
  78.3 7.2 %all-to-all-start.3 = ((bf16[8,32,864]{2,1,0:T(8,128)(2,1)}), bf16[8,32,864]{2,1,0:T(8,128)(2,1)S(1)}, u32[]{:S(2)}, u32[]{:S(2)}) async-start(bf16[8,32,864]{2,1,0:T(8,128)(2,1)} %pad_maximum_fusion), calls=%async_computation.3 | async-start | bytes 917504 | tf_op jit(solution)/shard_map/all_to_all | solution.py:56
  85.5 0.1 reduce_sum.41
  85.6 45.9 %all-gather = bf16[512,160]{1,0:T(8,128)(2,1)S(1)} all-gather(bf16[32,160]{1,0:T(8,128)(2,1)S(1)} %reduce_sum.41), channel_id=2, replica_groups=mesh['grp'=16,'shard'=32] {'grp'}, dimensions={0}, use_global_device_ids=true | all-gather | bytes 174080 | tf_op jit(solution)/shard_map/all_gather | solution.py:61
  131.5 0.1 copy.24
  131.6 0.3 broadcast_in_dim.20
  131.9 0.0 all-to-all-done.3
  132.0 1.8 broadcast_in_dim.21
  133.7 7.2 %all-to-all-start.1 = ((bf16[16,32,2560]{2,1,0:T(8,128)(2,1)}), bf16[16,32,2560]{2,1,0:T(8,128)(2,1)}, u32[]{:S(2)}, u32[]{:S(2)}) async-start(bf16[16,32,2560]{2,1,0:T(8,128)(2,1)} %broadcast_in_dim.21), calls=%async_computation.1 | async-start | bytes 5242880 | tf_op jit(solution)/shard_map/all_to_all | solution.py:18
  141.0 1.9 collective-permute-start
  142.9 0.1 reduce_sum.42
  143.0 34.5 %all_gather.12 = bf16[512,864]{1,0:T(8,128)(2,1)S(1)} all-gather(bf16[32,864]{1,0:T(8,128)(2,1)S(1)} %reduce_sum.42), channel_id=1, replica_groups=mesh['grp'=16,'shard'=32] {'grp'}, dimensions={0}, use_global_device_ids=true | all-gather | bytes 940032 | tf_op jit(solution)/shard_map/all_gather | solution.py:64
  177.5 0.5 copy.27
  178.0 0.0 collective-permute-done
  178.0 0.0 all-to-all-done.1
  178.0 5.6 %multiply_reduce_fusion = f32[512]{0:T(512)S(1)} fusion(bf16[512,864]{0,1:T(8,128)(2,1)S(1)} %copy.27, bf16[512,2560]{1,0:T(8,128)(2,1)} %bitcast.3, bf16[432,2560]{1,0:T(8,128)(2,1)} %collective-permute-done, bf16[432,2560]{1,0:T(8,128)(2,1)} %bitcast.5), kind=kOutput, calls=%fused_computation.4 | convolution fusion | flops 2275098112 | bytes 7931904 | tf_op jit(solution)/shard_map/dot_general | solution.py:13
  183.6 0.1 broadcast_in_dim.23
  183.7 0.1 reshape.41
  183.8 13.1 %all_to_all.25 = f32[16,1,256]{2,1,0:T(1,128)S(1)} all-to-all(f32[16,1,256]{2,1,0:T(1,128)S(1)} %reshape.41), channel_id=1, replica_groups={{0,2,4,6,8,10,12,14,16,18,20,22,24,26,28,30},{1,3,5,7,9,11,13,15,17,19,..., dimensions={0} | all-to-all | bytes 32768 | tf_op jit(solution)/shard_map/all_to_all | solution.py:69
  196.9 0.5 broadcast.2
  197.4 0.7 reduce.2
  198.1 0.1 reshape.42
  198.2 0.5 reduce_sum.44
  (2 shorter events, 0.0 us)
Async XLA Ops:
  0.0 50.4 %copy-start = (bf16[160,160]{1,0:T(8,128)(2,1)S(1)}, bf16[160,160]{1,0:T(8,128)(2,1)}, u32[]{:S(2)}) copy-start(bf16[160,160]{1,0:T(8,128)(2,1)} %param.7) | copy-start | bytes 153604
  2.4 11.5 %copy-start.2 = (bf16[64,160]{1,0:T(8,128)(2,1)S(1)}, bf16[64,160]{1,0:T(8,128)(2,1)}, u32[]{:S(2)}) copy-start(bf16[64,160]{1,0:T(8,128)(2,1)} %param.5) | copy-start | bytes 61444
  2.4 49.3 %all-to-all-start.2 = ((bf16[16,32,1728]{2,1,0:T(8,128)(2,1)}), bf16[16,32,1728]{2,1,0:T(8,128)(2,1)S(1)}, u32[]{:S(2)}, u32[]{:S(2)}) async-start(bf16[16,32,1728]{2,1,0:T(8,128)(2,1)} %broadcast_in_dim.22), calls=%async_computation.2 | async-start | bytes 3670016 | tf_op jit(solution)/shard_map/all_to_all | solution.py:18
  11.9 47.4 %collective-permute-start.2 = (bf16[432,1728]{1,0:T(8,128)(2,1)}, bf16[432,1728]{1,0:T(8,128)(2,1)}, u32[]{:S(2)}, u32[]{:S(2)}) collective-permute-start(bf16[432,1728]{1,0:T(8,128)(2,1)} %bitcast.11), channel_id=1, source_target_pairs={{0,1},{1,0},{2,3},{3,2},{4,5},{5,4},{6,7},{7,6},{8,9},{9,8},{10,11... | collective-permute-start | bytes 4478984 | tf_op jit(solution)/shard_map/ppermute | solution.py:37
  51.7 26.6 %all-to-all-start = ((f32[32,32,160]{2,1,0:T(8,128)}), f32[32,32,160]{2,1,0:T(8,128)S(1)}, u32[]{:S(2)}, u32[]{:S(2)}) async-start(f32[32,32,160]{2,1,0:T(8,128)} %bitcast.28), calls=%async_computation | async-start | bytes 2097152 | tf_op jit(solution)/shard_map/all_to_all | solution.py:43
  59.3 12.9 %copy-start.1 = (bf16[8,1,32,1728]{3,2,1,0:T(8,128)(2,1)}, bf16[8,1,32,1728]{3,2,1,0:T(8,128)(2,1)S(1)}, u32[]{:S(2)}) copy-start(bf16[8,1,32,1728]{3,2,1,0:T(8,128)(2,1)S(1)} %get-tuple-element.6) | copy-start | bytes 2654212
  61.6 10.6 %collective-permute-start.3 = (bf16[256,432]{0,1:T(8,128)(2,1)S(1)}, bf16[256,432]{0,1:T(8,128)(2,1)S(1)}, u32[]{:S(2)}, u32[]{:S(2)}) collective-permute-start(bf16[256,432]{0,1:T(8,128)(2,1)S(1)} %convolution_convert_fusion), channel_id=1, source_target_pairs={{0,480},{32,64},{64,32},{96,128},{128,96},{160,192},{192,160},{224... | collective-permute-start | bytes 663560 | tf_op jit(solution)/shard_map/ppermute | solution.py:51
  65.6 9.3 %collective-permute-start.1 = (bf16[256,432]{0,1:T(8,128)(2,1)S(1)}, bf16[256,432]{0,1:T(8,128)(2,1)S(1)}, u32[]{:S(2)}, u32[]{:S(2)}) collective-permute-start(bf16[256,432]{0,1:T(8,128)(2,1)S(1)} %convolution_convert_fusion.1), channel_id=1, source_target_pairs={{0,32},{32,0},{64,96},{96,64},{128,160},{160,128},{192,224},{224,1... | collective-permute-start | bytes 663560 | tf_op jit(solution)/shard_map/ppermute | solution.py:50
  78.3 53.7 %all-to-all-start.3 = ((bf16[8,32,864]{2,1,0:T(8,128)(2,1)}), bf16[8,32,864]{2,1,0:T(8,128)(2,1)S(1)}, u32[]{:S(2)}, u32[]{:S(2)}) async-start(bf16[8,32,864]{2,1,0:T(8,128)(2,1)} %pad_maximum_fusion), calls=%async_computation.3 | async-start | bytes 917504 | tf_op jit(solution)/shard_map/all_to_all | solution.py:56
  133.7 44.3 %all-to-all-start.1 = ((bf16[16,32,2560]{2,1,0:T(8,128)(2,1)}), bf16[16,32,2560]{2,1,0:T(8,128)(2,1)}, u32[]{:S(2)}, u32[]{:S(2)}) async-start(bf16[16,32,2560]{2,1,0:T(8,128)(2,1)} %broadcast_in_dim.21), calls=%async_computation.1 | async-start | bytes 5242880 | tf_op jit(solution)/shard_map/all_to_all | solution.py:18
  141.0 37.0 %collective-permute-start = (bf16[432,2560]{1,0:T(8,128)(2,1)}, bf16[432,2560]{1,0:T(8,128)(2,1)}, u32[]{:S(2)}, u32[]{:S(2)}) collective-permute-start(bf16[432,2560]{1,0:T(8,128)(2,1)} %bitcast.5), channel_id=1, source_target_pairs={{0,1},{1,0},{2,3},{3,2},{4,5},{5,4},{6,7},{7,6},{8,9},{9,8},{10,11... | collective-permute-start | bytes 6635528 | tf_op jit(solution)/shard_map/ppermute | solution.py:39

commit v2 on v1

v2 whole, which is shorter than its diff:
```python
import functools

import jax
import jax.numpy as jnp
from jax import lax
from jax.experimental import pallas as pl
from jax.experimental.pallas import tpu as pltpu
from jax.sharding import PartitionSpec as P


F32 = jnp.float32
BF16 = jnp.bfloat16
NT = (((1,), (1,)), ((), ()))


def product(left, right):
    return lax.dot_general(left, right, NT, preferred_element_type=F32)


def spread(block, axis, count, groups):
    copies = jnp.broadcast_to(block[None], (count, *block.shape))
    return lax.all_to_all(copies, axis, 0, 0, axis_index_groups=groups)


CUT = 512


def terms_kernel(quads, few, parity_ref, grads_ref, own_hbm, other_hbm, keep_ref, low_ref, high_ref, basis, terms, sems):
    cols = own_hbm.shape[0]
    first = pltpu.make_async_copy(own_hbm, basis.at[:cols], sems.at[0])
    second = pltpu.make_async_copy(other_hbm, basis.at[cols:], sems.at[1])
    first.start()
    second.start()
    first.wait()
    second.wait()
    terms[...] = product(grads_ref[...], basis[...])
    parity = parity_ref[0]
    for block in range(2 * quads):
        quad, pair = block // 2, block % 2

        def rows_of(which):
            rows = []
            for at in range(4):
                start = ((quad * 4 + at) * 4 + pair * 2) * few
                rows.append(terms[pl.ds(pl.multiple_of(start + which * few, few), few), :])
            return jnp.concatenate(rows, axis=0)

        keep_ref[block] = rows_of(parity)
        passed = rows_of(1 - parity).astype(BF16)
        low_ref[block] = passed[:, :CUT]
        high_ref[block] = passed[:, CUT:]


def out_terms(parity, grads, own, other, quads, few):
    blocks, rows, cols = 2 * quads, 4 * few, 2 * own.shape[0]
    smem, vmem = pl.BlockSpec(memory_space=pltpu.SMEM), pl.BlockSpec(memory_space=pltpu.VMEM)
    hbm = pl.BlockSpec(memory_space=pl.ANY)
    flops = 2 * grads.shape[0] * grads.shape[1] * cols
    return pl.pallas_call(
        functools.partial(terms_kernel, quads, few),
        out_shape=(
            jax.ShapeDtypeStruct((blocks, rows, cols), F32),
            jax.ShapeDtypeStruct((blocks, rows, CUT), BF16),
            jax.ShapeDtypeStruct((blocks, rows, cols - CUT), BF16),
        ),
        in_specs=[smem, vmem, hbm, hbm],
        out_specs=(vmem, vmem, vmem),
        scratch_shapes=[
            pltpu.VMEM((cols, grads.shape[1]), BF16),
            pltpu.VMEM((grads.shape[0], cols), F32),
            pltpu.SemaphoreType.DMA((2,)),
        ],
        cost_estimate=pl.CostEstimate(flops=flops, bytes_accessed=6 << 20, transcendentals=0),
        name="out_terms",
    )(parity, grads, own, other)


def message_kernel(wide, parity_ref, keep_ref, low_ref, high_ref, own_ref, near_ref, sent_ref):
    odd = parity_ref[0] == 1
    own, near = own_ref[...].astype(F32), near_ref[...].astype(F32)
    act = jnp.concatenate([jnp.where(odd, near, own), jnp.where(odd, own, near)], axis=0)
    rest = act[:, wide:]
    blank = jnp.zeros((act.shape[0], 2 * wide - act.shape[1]), F32)
    act = jnp.concatenate([act[:, :wide], jnp.concatenate([rest, blank], axis=1)], axis=0)
    act = act.astype(BF16)
    for block in range(keep_ref.shape[0]):
        sent_ref[block, :, :wide] = act
        low = keep_ref[block, :, :CUT] + low_ref[block].astype(F32)
        sent_ref[block, :, wide : wide + CUT] = low.astype(BF16)
        high = keep_ref[block, :, CUT:] + high_ref[block].astype(F32)
        sent_ref[block, :, wide + CUT :] = high.astype(BF16)


def message(parity, keep, low, high, own, near, wide):
    smem, vmem = pl.BlockSpec(memory_space=pltpu.SMEM), pl.BlockSpec(memory_space=pltpu.VMEM)
    shape = (*keep.shape[:2], wide + keep.shape[2])
    return pl.pallas_call(
        functools.partial(message_kernel, wide),
        out_shape=jax.ShapeDtypeStruct(shape, BF16),
        in_specs=[smem] + [vmem] * 5,
        out_specs=vmem,
        cost_estimate=pl.CostEstimate(flops=1 << 20, bytes_accessed=2 << 20, transcendentals=0),
        name="message",
    )(parity, keep, low, high, own, near)


def local(activations, grad_outputs, basis_in, basis_out, query_grads):
    n_grp = lax.axis_size("grp")
    n_shard = lax.axis_size("shard")
    chips = n_shard // 2
    one_core = [[2 * chip + core for chip in range(chips)] for core in range(2)]
    other_core = [(at, at ^ 1) for at in range(n_shard)]
    pairs = [(at, at ^ 1) for at in range(n_grp)]
    cross_pairs = [(at, (at + (1 if at % 2 else -1)) % n_grp) for at in range(n_grp)]
    alike = [list(range(parity, n_grp, 2)) for parity in range(2)]
    quads = n_grp // 4
    far = [list(range(at, n_grp, 4)) for at in range(4)]
    rows = grad_outputs.shape[0]
    few = rows // 4
    half = chips * rows
    eig = 4 * basis_in.shape[1]
    place = lax.axis_index("grp")
    parity = place & 1

    grads = spread(grad_outputs, "shard", chips, one_core).reshape(half, -1)
    basis_own = basis_out.T
    basis_other = lax.ppermute(basis_own, "shard", other_core)
    query_own = query_grads[0].T
    query_other = lax.ppermute(query_own, "shard", other_core)

    near = [basis_in]
    for at in range(1, 4):
        near.append(lax.ppermute(basis_in, "grp", [(to, to ^ at) for to in range(n_grp)]))
    odd = parity == 1
    near = [jnp.where(odd, near[at ^ 1], near[at]) for at in range(4)]
    late = (place & 2) == 2
    near = [jnp.where(late, near[at ^ 2], near[at]) for at in range(4)]
    basis = jnp.concatenate(near, axis=1)
    acts = activations.reshape(2, 4, few, -1).transpose(1, 0, 2, 3).reshape(2 * rows, -1)
    acts = lax.all_gather(acts, "grp", axis=0, tiled=True, axis_index_groups=far)
    act_terms = jnp.dot(acts, basis, preferred_element_type=F32)
    act_terms = lax.all_to_all(act_terms.reshape(n_shard, few, eig), "shard", 0, 0)
    act_own = jnp.sum(act_terms, axis=0).astype(BF16)
    act_near = lax.ppermute(act_own, "grp", pairs)

    parity_at = parity.astype(jnp.int32).reshape(1)
    keep, low, high = out_terms(parity_at, grads, basis_own, basis_other, quads, few)
    low = lax.ppermute(low, "grp", pairs)
    high = lax.ppermute(high, "grp", cross_pairs)

    wide = -(-eig // 256) * 128
    skip = 2 * wide - eig
    sent = message(parity_at, keep, low, high, act_own, act_near, wide)
    got = lax.all_to_all(sent, "grp", 0, 0, axis_index_groups=alike)
    out_own = jnp.sum(got[:, :, wide:].astype(F32), axis=0).astype(BF16)
    act_rot = jnp.concatenate([got[:, : 2 * few, :wide], got[:, 2 * few :, : wide - skip]], axis=2)
    act_rot = act_rot.reshape(quads, 2, 2 * few, eig).transpose(1, 2, 0, 3)
    act_rot = act_rot.reshape(rows, quads * eig)
    act_rot = spread(act_rot, "shard", chips, one_core).reshape(half, quads * eig)
    out_rot = lax.all_gather(out_own, "grp", axis=0, tiled=True)

    query = jnp.concatenate([query_own, query_other], axis=0)
    partial = jnp.sum(product(act_rot, query) * out_rot.astype(F32), axis=1)
    partial = partial.reshape(quads, 4, 4, few).transpose(0, 2, 1, 3).reshape(chips, 1, rows)
    partial = jnp.pad(partial, ((0, 0), (0, 7), (0, 128 - rows)))
    partial = lax.all_to_all(partial, "shard", 0, 0, axis_index_groups=one_core)
    return jnp.sum(partial, axis=0)[:1, :rows]


def solution(mesh):
    placed = (
        P("grp", "shard"),
        P("shard", "grp"),
        P("shard", "grp"),
        P("grp", "shard"),
        P("grp", None, "shard"),
    )
    return jax.shard_map(
        local, mesh=mesh, in_specs=placed, out_specs=P("grp", "shard"), check_vma=False
    )
```

time: 200 us -> 188 us (0.940)
  the two profiles are of different devices: /device:TPU:2 before, /device:TPU:32 now
where the time goes in v2:
time: 188 us; the launch traced here: 187 us
  blocking collectives  116 us (62%)
  starting transfers between devices  45.8 us (24%)
  Pallas kernels  8.86 us (5%)
  local copies, waits for them, and re-layouts  7.04 us (4%)
  matrix products  6.2 us (3%)
  waiting for transfers between devices  2.42 us (1%)
    all_to_all x1, blocking collectives, local(): got = lax.all_to_all(sent, 'grp', 0, 0, axis_index_groups=alike)  43.4 us
    all_gather x1, blocking collectives, local(): out_rot = lax.all_gather(out_own, 'grp', axis=0, tiled=True)  33.7 us
    all_gather x1, blocking collectives, local(): lax.all_gather(acts, 'grp', axis=0, tiled=True, axis_index_groups=far)  24.2 us
    all_to_all x1, blocking collectives, local(): partial = lax.all_to_all(partial, 'shard', 0, 0, axis_index_groups=one_core)  14.7 us
    all_to_all x2, starting transfers between devices, spread(): return lax.all_to_all(copies, axis, 0, 0, axis_index_groups=groups)  14 us
    ppermute x3, starting transfers between devices, local(): lax.ppermute(basis_in, 'grp', [(to, to ^ at) for to in range(n_grp)])  10.5 us
    all_to_all x1, starting transfers between devices, local(): lax.all_to_all(act_terms.reshape(n_shard, few, eig), 'shard', 0, 0)  7.49 us
    pallas_call x1, Pallas kernels, out_terms(): pl.pallas_call(functools.partial(terms_kernel, quads, few), out_shape=(ja...  6.62 us
  transfers between devices with their start and end apart: 11, of which 1 were waited for; matrix products, arithmetic and copies ran while one was open for 1% of the time, Pallas kernels for 4%

profile of v2, /device:TPU:32, one launch (start us, length us, event | category | flops | bytes accessed | tf_op | source)
XLA Modules:
  0.0 186.9 jit_solution(6321839065216327832)
XLA Ops:
  0.0 2.3 %broadcast_in_dim.6 = bf16[16,32,1728]{2,1,0:T(8,128)(2,1)} broadcast(bf16[32,1728]{1,0:T(8,128)(2,1)} %param.6), dimensions={1,2} | broadcast | bytes 1880064 | tf_op jit(solution)/shard_map/broadcast_in_dim | solution.py:21
  2.3 0.0 copy-start.3
  2.3 0.0 copy-start.5
  2.3 7.2 %all-to-all-start = ((bf16[16,32,1728]{2,1,0:T(8,128)(2,1)}), bf16[16,32,1728]{2,1,0:T(8,128)(2,1)S(1)}, u32[]{:S(2)}, u32[]{:S(2)}) async-start(bf16[16,32,1728]{2,1,0:T(8,128)(2,1)} %broadcast_in_dim.6), calls=%async_computation | async-start | bytes 3670016 | tf_op jit(solution)/shard_map/all_to_all | solution.py:22
  9.5 1.9 %collective-permute-start = (bf16[432,1728]{1,0:T(8,128)(2,1)}, bf16[432,1728]{1,0:T(8,128)(2,1)}, u32[]{:S(2)}, u32[]{:S(2)}) collective-permute-start(bf16[432,1728]{1,0:T(8,128)(2,1)} %bitcast.35), channel_id=1, source_target_pairs={{0,1},{1,0},{2,3},{3,2},{4,5},{5,4},{6,7},{7,6},{8,9},{9,8},{10,11... | collective-permute-start | bytes 4478984 | tf_op jit(solution)/shard_map/ppermute | solution.py:127
  11.5 0.0 copy-done.3
  11.5 3.8 %collective-permute-start.3 = (bf16[160,160]{1,0:T(8,128)(2,1)S(1)}, bf16[160,160]{1,0:T(8,128)(2,1)S(1)}, u32[]{:S(2)}, u32[]{:S(2)}) collective-permute-start(bf16[160,160]{1,0:T(8,128)(2,1)S(1)} %copy-done.3), channel_id=1, source_target_pairs={{0,96},{32,64},{64,32},{96,0},{128,224},{160,192},{192,160},{224,1... | collective-permute-start | bytes 153608 | tf_op jit(solution)/shard_map/ppermute | solution.py:133
  15.3 4.5 %collective-permute-start.4 = (bf16[160,160]{1,0:T(8,128)(2,1)S(1)}, bf16[160,160]{1,0:T(8,128)(2,1)S(1)}, u32[]{:S(2)}, u32[]{:S(2)}) collective-permute-start(bf16[160,160]{1,0:T(8,128)(2,1)S(1)} %copy-done.3), channel_id=1, source_target_pairs={{0,64},{32,96},{64,0},{96,32},{128,192},{160,224},{192,128},{224,1... | collective-permute-start | bytes 153608 | tf_op jit(solution)/shard_map/ppermute | solution.py:133
  19.8 2.2 %collective-permute-start.5 = (bf16[160,160]{1,0:T(8,128)(2,1)S(1)}, bf16[160,160]{1,0:T(8,128)(2,1)S(1)}, u32[]{:S(2)}, u32[]{:S(2)}) collective-permute-start(bf16[160,160]{1,0:T(8,128)(2,1)S(1)} %copy-done.3), channel_id=1, source_target_pairs={{0,32},{32,0},{64,96},{96,64},{128,160},{160,128},{192,224},{224,1... | collective-permute-start | bytes 153608 | tf_op jit(solution)/shard_map/ppermute | solution.py:133
  22.0 0.0 copy-done.5
  22.0 24.2 %all_gather.6 = bf16[256,160]{1,0:T(8,128)(2,1)S(1)} all-gather(bf16[64,160]{1,0:T(8,128)(2,1)S(1)} %bitcast.29), channel_id=1, replica_groups={{0,128,256,384},{32,160,288,416},{64,192,320,448},{96,224,352,480},{1,1..., dimensions={0}, use_global_device_ids=true | all-gather | bytes 102400 | tf_op jit(solution)/shard_map/all_gather | solution.py:140
  46.2 0.0 collective-permute-done.3
  46.2 0.0 collective-permute-done.4
  46.2 0.0 collective-permute-done.5
  46.3 1.2 convolution_bitcast_fusion
  47.5 0.0 all-to-all-done
  47.5 0.0 copy-start
  47.5 7.5 %all-to-all-start.1 = ((f32[32,8,640]{2,1,0:T(8,128)}), f32[32,8,640]{2,1,0:T(8,128)S(1)}, u32[]{:S(2)}, u32[]{:S(2)}) async-start(f32[32,8,640]{2,1,0:T(8,128)} %convolution_bitcast_fusion), calls=%async_computation.1 | async-start | bytes 1310720 | tf_op jit(solution)/shard_map/all_to_all | solution.py:142
  55.0 0.0 collective-permute-done.other_hbm
  55.0 0.0 copy-done
  55.0 6.6 %out_terms.1 = (f32[8,32,864]{2,1,0:T(8,128)}, bf16[8,32,512]{2,1,0:T(8,128)(2,1)}, bf16[8,32,352]{2,1,0:T(8,128)(2,1)}) custom-call(s32[1]{0:T(128)} %bitcast.parity_ref, bf16[512,1728]{1,0:T(8,128)(2,1)} %bitcast.25, bf16[432,1728]{1,0:T(8,128)(2,1)} %bitcast.36, bf16[432,1728]{1,0:T(8,128)(2,1)} %collective-permute-done.other_hbm), custom_call_target="tpu_custom_call" | custom-call | flops 1528823808 | bytes 6291456 | tf_op jit(solution)/shard_map/out_terms/pallas_call | solution.py:59
  61.7 3.6 %collective-permute-start.1 = (bf16[8,32,512]{2,1,0:T(8,128)(2,1)}, bf16[8,32,512]{2,1,0:T(8,128)(2,1)S(1)}, u32[]{:S(2)}, u32[]{:S(2)}) collective-permute-start(bf16[8,32,512]{2,1,0:T(8,128)(2,1)} %get-tuple-element.9), channel_id=1, source_target_pairs={{0,32},{32,0},{64,96},{96,64},{128,160},{160,128},{192,224},{224,1... | collective-permute-start | bytes 786440 | tf_op jit(solution)/shard_map/ppermute | solution.py:148
  65.3 3.2 %collective-permute-start.2 = (bf16[8,32,352]{2,1,0:T(8,128)(2,1)}, bf16[8,32,352]{2,1,0:T(8,128)(2,1)S(1)}, u32[]{:S(2)}, u32[]{:S(2)}) collective-permute-start(bf16[8,32,352]{2,1,0:T(8,128)(2,1)} %get-tuple-element.10), channel_id=1, source_target_pairs={{0,480},{32,64},{64,32},{96,128},{128,96},{160,192},{192,160},{224... | collective-permute-start | bytes 540680 | tf_op jit(solution)/shard_map/ppermute | solution.py:149
  68.5 0.0 all-to-all-done.1
  68.5 0.1 reduce_sum.39.own_ref
  68.6 0.0 copy-start.4
  68.6 3.2 %collective-permute-start.6 = (bf16[8,640]{1,0:T(8,128)(2,1)S(1)}, bf16[8,640]{1,0:T(8,128)(2,1)S(1)}, u32[]{:S(2)}, u32[]{:S(2)}) collective-permute-start(bf16[8,640]{1,0:T(8,128)(2,1)S(1)} %reduce_sum.39.own_ref), channel_id=1, source_target_pairs={{0,32},{32,0},{64,96},{96,64},{128,160},{160,128},{192,224},{224,1... | collective-permute-start | bytes 30728 | tf_op jit(solution)/shard_map/ppermute | solution.py:144
  71.8 2.4 %collective-permute-done.6.near_ref = bf16[8,640]{1,0:T(8,128)(2,1)S(1)} collective-permute-done((bf16[8,640]{1,0:T(8,128)(2,1)S(1)}, bf16[8,640]{1,0:T(8,128)(2,1)S(1)}, u32[]{:S(2)}, u32[]{:S(2)}) %collective-permute-start.6) | collective-permute-done | bytes 10272 | tf_op jit(solution)/shard_map/ppermute | solution.py:144
  74.2 0.0 copy-start.6
  74.2 0.0 collective-permute-done.2.high_ref
  74.2 0.0 copy-start.2
  74.2 0.0 collective-permute-done.1.low_ref
  74.2 0.0 copy-start.1
  74.2 0.0 copy-done.4
  74.2 0.5 copy-done.6
  74.8 0.1 copy-done.2
  74.9 0.1 copy-done.1
  75.0 2.2 %message.1 = bf16[8,32,1248]{2,1,0:T(8,128)(2,1)} custom-call(s32[1]{0:T(128)} %bitcast.parity_ref, f32[8,32,864]{2,1,0:T(8,128)} %get-tuple-element.8.keep_ref, bf16[8,32,512]{2,1,0:T(8,128)(2,1)} %copy-done.1, bf16[8,32,352]{2,1,0:T(8,128)(2,1)} %copy-done.2, bf16[8,640]{1,0:T(8,128)(2,1)} %copy-done.4, bf16[8,640]{1,0:T(8,128)(2,1)} %copy-done.6), custom_call_target="tpu_custom_call" | custom-call | flops 1048576 | bytes 2097152 | tf_op jit(solution)/shard_map/message/pallas_call | solution.py:97
  77.2 43.4 %all_to_all.25 = bf16[8,32,1248]{2,1,0:T(8,128)(2,1)S(1)} all-to-all(bf16[8,32,1248]{2,1,0:T(8,128)(2,1)} %message.1), channel_id=1, replica_groups={{0,64,128,192,256,320,384,448},{32,96,160,224,288,352,416,480},{1,65,12..., dimensions={0} | all-to-all | bytes 1277952 | tf_op jit(solution)/shard_map/all_to_all | solution.py:154
  120.7 0.1 copy.11
  120.8 1.8 broadcast_in_dim.15
  122.6 6.8 %all-to-all-start.3 = ((bf16[16,32,2560]{2,1,0:T(8,128)(2,1)}), bf16[16,32,2560]{2,1,0:T(8,128)(2,1)S(1)}, u32[]{:S(2)}, u32[]{:S(2)}) async-start(bf16[16,32,2560]{2,1,0:T(8,128)(2,1)} %broadcast_in_dim.15), calls=%async_computation.3 | async-start | bytes 5242880 | tf_op jit(solution)/shard_map/all_to_all | solution.py:22
  129.4 1.9 %collective-permute-start.7 = (bf16[432,2560]{1,0:T(8,128)(2,1)}, bf16[432,2560]{1,0:T(8,128)(2,1)}, u32[]{:S(2)}, u32[]{:S(2)}) collective-permute-start(bf16[432,2560]{1,0:T(8,128)(2,1)} %bitcast.33), channel_id=1, source_target_pairs={{0,1},{1,0},{2,3},{3,2},{4,5},{5,4},{6,7},{7,6},{8,9},{9,8},{10,11... | collective-permute-start | bytes 6635528 | tf_op jit(solution)/shard_map/ppermute | solution.py:129
  131.4 0.1 slice_reduce_fusion
  131.4 33.7 %all_gather.7 = bf16[512,864]{1,0:T(8,128)(2,1)S(1)} all-gather(bf16[32,864]{1,0:T(8,128)(2,1)S(1)} %slice_reduce_fusion), channel_id=1, replica_groups=mesh['grp'=16,'shard'=32] {'grp'}, dimensions={0}, use_global_device_ids=true | all-gather | bytes 940032 | tf_op jit(solution)/shard_map/all_gather | solution.py:160
  165.2 1.3 copy.12
  166.5 0.0 collective-permute-done.7
  166.5 0.0 all-to-all-done.3
  166.5 5.0 %multiply_reduce_fusion = f32[512]{0:T(512)S(1)} fusion(bf16[512,864]{0,1:T(8,128)(2,1)} %copy.12, bf16[512,2560]{1,0:T(8,128)(2,1)S(1)} %bitcast.24, bf16[432,2560]{1,0:T(8,128)(2,1)} %collective-permute-done.7, bf16[432,2560]{1,0:T(8,128)(2,1)} %bitcast.34), kind=kOutput, calls=%fused_computation.4 | convolution fusion | flops 2275098112 | bytes 7931904 | tf_op jit(solution)/shard_map/dot_general | solution.py:17
  171.4 0.1 reshape.36
  171.6 0.1 reshape.37
  171.7 14.7 %all_to_all.26 = f32[16,8,128]{2,1,0:T(8,128)S(1)} all-to-all(f32[16,8,128]{2,1,0:T(8,128)S(1)} %pad.4.clone), channel_id=1, replica_groups={{0,2,4,6,8,10,12,14,16,18,20,22,24,26,28,30},{1,3,5,7,9,11,13,15,17,19,..., dimensions={0} | all-to-all | bytes 131072 | tf_op jit(solution)/shard_map/all_to_all | solution.py:166
  186.4 0.5 slice.15
  (9 shorter events, 0.1 us)
Async XLA Ops:
  2.3 9.1 %copy-start.3 = (bf16[160,160]{1,0:T(8,128)(2,1)S(1)}, bf16[160,160]{1,0:T(8,128)(2,1)}, u32[]{:S(2)}) copy-start(bf16[160,160]{1,0:T(8,128)(2,1)} %param.7) | copy-start | bytes 153604
  2.3 19.6 %copy-start.5 = (bf16[64,160]{1,0:T(8,128)(2,1)S(1)}, bf16[64,160]{1,0:T(8,128)(2,1)}, u32[]{:S(2)}) copy-start(bf16[64,160]{1,0:T(8,128)(2,1)} %param.5) | copy-start | bytes 61444
  2.3 45.2 %all-to-all-start = ((bf16[16,32,1728]{2,1,0:T(8,128)(2,1)}), bf16[16,32,1728]{2,1,0:T(8,128)(2,1)S(1)}, u32[]{:S(2)}, u32[]{:S(2)}) async-start(bf16[16,32,1728]{2,1,0:T(8,128)(2,1)} %broadcast_in_dim.6), calls=%async_computation | async-start | bytes 3670016 | tf_op jit(solution)/shard_map/all_to_all | solution.py:22
  9.5 45.5 %collective-permute-start = (bf16[432,1728]{1,0:T(8,128)(2,1)}, bf16[432,1728]{1,0:T(8,128)(2,1)}, u32[]{:S(2)}, u32[]{:S(2)}) collective-permute-start(bf16[432,1728]{1,0:T(8,128)(2,1)} %bitcast.35), channel_id=1, source_target_pairs={{0,1},{1,0},{2,3},{3,2},{4,5},{5,4},{6,7},{7,6},{8,9},{9,8},{10,11... | collective-permute-start | bytes 4478984 | tf_op jit(solution)/shard_map/ppermute | solution.py:127
  11.5 34.8 %collective-permute-start.3 = (bf16[160,160]{1,0:T(8,128)(2,1)S(1)}, bf16[160,160]{1,0:T(8,128)(2,1)S(1)}, u32[]{:S(2)}, u32[]{:S(2)}) collective-permute-start(bf16[160,160]{1,0:T(8,128)(2,1)S(1)} %copy-done.3), channel_id=1, source_target_pairs={{0,96},{32,64},{64,32},{96,0},{128,224},{160,192},{192,160},{224,1... | collective-permute-start | bytes 153608 | tf_op jit(solution)/shard_map/ppermute | solution.py:133
  15.3 30.9 %collective-permute-start.4 = (bf16[160,160]{1,0:T(8,128)(2,1)S(1)}, bf16[160,160]{1,0:T(8,128)(2,1)S(1)}, u32[]{:S(2)}, u32[]{:S(2)}) collective-permute-start(bf16[160,160]{1,0:T(8,128)(2,1)S(1)} %copy-done.3), channel_id=1, source_target_pairs={{0,64},{32,96},{64,0},{96,32},{128,192},{160,224},{192,128},{224,1... | collective-permute-start | bytes 153608 | tf_op jit(solution)/shard_map/ppermute | solution.py:133
  19.8 26.5 %collective-permute-start.5 = (bf16[160,160]{1,0:T(8,128)(2,1)S(1)}, bf16[160,160]{1,0:T(8,128)(2,1)S(1)}, u32[]{:S(2)}, u32[]{:S(2)}) collective-permute-start(bf16[160,160]{1,0:T(8,128)(2,1)S(1)} %copy-done.3), channel_id=1, source_target_pairs={{0,32},{32,0},{64,96},{96,64},{128,160},{160,128},{192,224},{224,1... | collective-permute-start | bytes 153608 | tf_op jit(solution)/shard_map/ppermute | solution.py:133
  47.5 7.5 %copy-start = (bf16[16,32,1728]{2,1,0:T(8,128)(2,1)}, bf16[16,32,1728]{2,1,0:T(8,128)(2,1)S(1)}, u32[]{:S(2)}) copy-start(bf16[16,32,1728]{2,1,0:T(8,128)(2,1)S(1)} %all-to-all-done) | copy-start | bytes 5308420
  47.5 21.0 %all-to-all-start.1 = ((f32[32,8,640]{2,1,0:T(8,128)}), f32[32,8,640]{2,1,0:T(8,128)S(1)}, u32[]{:S(2)}, u32[]{:S(2)}) async-start(f32[32,8,640]{2,1,0:T(8,128)} %convolution_bitcast_fusion), calls=%async_computation.1 | async-start | bytes 1310720 | tf_op jit(solution)/shard_map/all_to_all | solution.py:142
  61.7 12.6 %collective-permute-start.1 = (bf16[8,32,512]{2,1,0:T(8,128)(2,1)}, bf16[8,32,512]{2,1,0:T(8,128)(2,1)S(1)}, u32[]{:S(2)}, u32[]{:S(2)}) collective-permute-start(bf16[8,32,512]{2,1,0:T(8,128)(2,1)} %get-tuple-element.9), channel_id=1, source_target_pairs={{0,32},{32,0},{64,96},{96,64},{128,160},{160,128},{192,224},{224,1... | collective-permute-start | bytes 786440 | tf_op jit(solution)/shard_map/ppermute | solution.py:148
  65.3 8.9 %collective-permute-start.2 = (bf16[8,32,352]{2,1,0:T(8,128)(2,1)}, bf16[8,32,352]{2,1,0:T(8,128)(2,1)S(1)}, u32[]{:S(2)}, u32[]{:S(2)}) collective-permute-start(bf16[8,32,352]{2,1,0:T(8,128)(2,1)} %get-tuple-element.10), channel_id=1, source_target_pairs={{0,480},{32,64},{64,32},{96,128},{128,96},{160,192},{192,160},{224... | collective-permute-start | bytes 540680 | tf_op jit(solution)/shard_map/ppermute | solution.py:149
  68.6 5.6 %copy-start.4 = (bf16[8,640]{1,0:T(8,128)(2,1)}, bf16[8,640]{1,0:T(8,128)(2,1)S(1)}, u32[]{:S(2)}) copy-start(bf16[8,640]{1,0:T(8,128)(2,1)S(1)} %reduce_sum.39.own_ref) | copy-start | bytes 30724
  68.6 5.6 %collective-permute-start.6 = (bf16[8,640]{1,0:T(8,128)(2,1)S(1)}, bf16[8,640]{1,0:T(8,128)(2,1)S(1)}, u32[]{:S(2)}, u32[]{:S(2)}) collective-permute-start(bf16[8,640]{1,0:T(8,128)(2,1)S(1)} %reduce_sum.39.own_ref), channel_id=1, source_target_pairs={{0,32},{32,0},{64,96},{96,64},{128,160},{160,128},{192,224},{224,1... | collective-permute-start | bytes 30728 | tf_op jit(solution)/shard_map/ppermute | solution.py:144
  74.2 0.6 copy-start.6
  74.2 0.7 copy-start.2
  74.2 0.8 copy-start.1
  122.6 43.9 %all-to-all-start.3 = ((bf16[16,32,2560]{2,1,0:T(8,128)(2,1)}), bf16[16,32,2560]{2,1,0:T(8,128)(2,1)S(1)}, u32[]{:S(2)}, u32[]{:S(2)}) async-start(bf16[16,32,2560]{2,1,0:T(8,128)(2,1)} %broadcast_in_dim.15), calls=%async_computation.3 | async-start | bytes 5242880 | tf_op jit(solution)/shard_map/all_to_all | solution.py:22
  129.4 37.0 %collective-permute-start.7 = (bf16[432,2560]{1,0:T(8,128)(2,1)}, bf16[432,2560]{1,0:T(8,128)(2,1)}, u32[]{:S(2)}, u32[]{:S(2)}) collective-permute-start(bf16[432,2560]{1,0:T(8,128)(2,1)} %bitcast.33), channel_id=1, source_target_pairs={{0,1},{1,0},{2,3},{3,2},{4,5},{5,4},{6,7},{7,6},{8,9},{9,8},{10,11... | collective-permute-start | bytes 6635528 | tf_op jit(solution)/shard_map/ppermute | solution.py:129

commit v3 on v2

--- a/solution.py
+++ b/solution.py
@@ -25,30 +25,34 @@
 CUT = 512
 
 
-def terms_kernel(quads, few, parity_ref, grads_ref, own_hbm, other_hbm, keep_ref, low_ref, high_ref, basis, terms, sems):
+def terms_kernel(quads, few, parity_ref, grads_ref, own_hbm, other_hbm, keep_ref, low_ref, high_ref, basis, sems):
     cols = own_hbm.shape[0]
     first = pltpu.make_async_copy(own_hbm, basis.at[:cols], sems.at[0])
     second = pltpu.make_async_copy(other_hbm, basis.at[cols:], sems.at[1])
     first.start()
     second.start()
+    odd = parity_ref[0] == 1
+
+    def put(start, stop):
+        terms = product(grads_ref[...], basis[start:stop])
+        for block in range(2 * quads):
+            quad, pair = block // 2, block % 2
+            halves = []
+            for which in range(2):
+                begins = [((quad * 4 + at) * 4 + pair * 2 + which) * few for at in range(4)]
+                halves.append(jnp.concatenate([terms[at : at + few] for at in begins], axis=0))
+            keep_ref[block, :, start:stop] = jnp.where(odd, halves[1], halves[0])
+            passed = jnp.where(odd, halves[0], halves[1]).astype(BF16)
+            if stop <= CUT:
+                low_ref[block, :, start:stop] = passed
+            else:
+                high_ref[block, :, start - CUT : stop - CUT] = passed
+
     first.wait()
+    put(0, 384)
     second.wait()
-    terms[...] = product(grads_ref[...], basis[...])
-    parity = parity_ref[0]
-    for block in range(2 * quads):
-        quad, pair = block // 2, block % 2
-
-        def rows_of(which):
-            rows = []
-            for at in range(4):
-                start = ((quad * 4 + at) * 4 + pair * 2) * few
-                rows.append(terms[pl.ds(pl.multiple_of(start + which * few, few), few), :])
-            return jnp.concatenate(rows, axis=0)
-
-        keep_ref[block] = rows_of(parity)
-        passed = rows_of(1 - parity).astype(BF16)
-        low_ref[block] = passed[:, :CUT]
-        high_ref[block] = passed[:, CUT:]
+    put(384, CUT)
+    put(CUT, 2 * cols)
 
 
 def out_terms(parity, grads, own, other, quads, few):
@@ -67,7 +71,6 @@
         out_specs=(vmem, vmem, vmem),
         scratch_shapes=[
             pltpu.VMEM((cols, grads.shape[1]), BF16),
-            pltpu.VMEM((grads.shape[0], cols), F32),
             pltpu.SemaphoreType.DMA((2,)),
         ],
         cost_estimate=pl.CostEstimate(flops=flops, bytes_accessed=6 << 20, transcendentals=0),
@@ -102,6 +105,81 @@
         cost_estimate=pl.CostEstimate(flops=1 << 20, bytes_accessed=2 << 20, transcendentals=0),
         name="message",
     )(parity, keep, low, high, own, near)
+
+
+def scores_kernel(quads, few, act_hbm, own_hbm, other_hbm, out_hbm, part_ref, act, query, out, sems):
+    rows, cols, half = act.shape[0] // 4, query.shape[0], own_hbm.shape[0]
+    blocks = [pl.ds(at * rows, rows) for at in range(4)]
+    steps = [(at, min(at + 256, cols)) for at in range(0, cols, 256)]
+    cuts = sorted({0, half, cols} | {at for at, _ in steps})
+    loads = []
+    for at, to in zip(cuts[:-1], cuts[1:], strict=True):
+        source = own_hbm.at[at:to] if to <= half else other_hbm.at[at - half : to - half]
+        copy = pltpu.make_async_copy(source, query.at[at:to], sems.at[len(loads)])
+        loads.append((to, copy))
+    acts = []
+    for at, block in enumerate(blocks):
+        sem = sems.at[len(loads) + at]
+        acts.append(pltpu.make_async_copy(act_hbm.at[block], act.at[block], sem))
+    outs = pltpu.make_async_copy(out_hbm, out, sems.at[len(loads) + 4])
+    loads[0][1].start()
+    for copy in (*acts, outs):
+        copy.start()
+    for _, copy in loads[1:]:
+        copy.start()
+
+    ready = 0
+    totals = [jnp.zeros((rows, 128), F32)] * 4
+    for start, stop in steps:
+        while ready < len(loads) and (ready == 0 or loads[ready - 1][0] < stop):
+            loads[ready][1].wait()
+            ready += 1
+        for at, block in enumerate(blocks):
+            if start == 0:
+                acts[at].wait()
+            terms = product(act[block], query[start:stop])
+            if start == 0 and at == 0:
+                outs.wait()
+            terms = terms * out[block, start:stop].astype(F32)
+            for lane in range(0, stop - start, 128):
+                piece = terms[:, lane : lane + 128]
+                short = 128 - piece.shape[1]
+                if short:
+                    piece = jnp.concatenate([piece, jnp.zeros((rows, short), F32)], axis=1)
+                totals[at] = totals[at] + piece
+
+    total = jnp.concatenate(totals, axis=0)
+    moved = []
+    for quad in range(quads):
+        for second in range(4):
+            for third in range(4):
+                at = ((quad * 4 + third) * 4 + second) * few
+                moved.append(total[at : at + few])
+    line = jnp.sum(jnp.concatenate(moved, axis=0).T, axis=0, keepdims=True)
+    part_ref[...] = jnp.zeros_like(part_ref)
+    for at in range(part_ref.shape[0]):
+        part_ref[at, :1, : 4 * few] = line[:, at * 4 * few : (at + 1) * 4 * few]
+
+
+def part_scores(act, own, other, out, quads, few):
+    hbm = pl.BlockSpec(memory_space=pl.ANY)
+    cols = 2 * own.shape[0]
+    flops = 2 * act.shape[0] * act.shape[1] * cols
+    return pl.pallas_call(
+        functools.partial(scores_kernel, quads, few),
+        out_shape=jax.ShapeDtypeStruct((act.shape[0] // (4 * few), 8, 128), F32),
+        in_specs=[hbm] * 4,
+        out_specs=pl.BlockSpec(memory_space=pltpu.VMEM),
+        scratch_shapes=[
+            pltpu.VMEM(act.shape, BF16),
+            pltpu.VMEM((cols, act.shape[1]), BF16),
+            pltpu.VMEM(out.shape, BF16),
+            pltpu.SemaphoreType.DMA((10,)),
+        ],
+        cost_estimate=pl.CostEstimate(flops=flops, bytes_accessed=8 << 20, transcendentals=0),
+        compiler_params=pltpu.CompilerParams(vmem_limit_bytes=66_000_000),
+        name="part_scores",
+    )(act, own, other, out)
 
 
 def local(activations, grad_outputs, basis_in, basis_out, query_grads):
@@ -159,10 +237,7 @@
     act_rot = spread(act_rot, "shard", chips, one_core).reshape(half, quads * eig)
     out_rot = lax.all_gather(out_own, "grp", axis=0, tiled=True)
 
-    query = jnp.concatenate([query_own, query_other], axis=0)
-    partial = jnp.sum(product(act_rot, query) * out_rot.astype(F32), axis=1)
-    partial = partial.reshape(quads, 4, 4, few).transpose(0, 2, 1, 3).reshape(chips, 1, rows)
-    partial = jnp.pad(partial, ((0, 0), (0, 7), (0, 128 - rows)))
+    partial = part_scores(act_rot, query_own, query_other, out_rot, quads, few)
     partial = lax.all_to_all(partial, "shard", 0, 0, axis_index_groups=one_core)
     return jnp.sum(partial, axis=0)[:1, :rows]
 

time: 188 us -> 195 us (1.037)
  Pallas kernels: 8.86 us -> 19.9 us
  matrix products: 6.2 us -> 1.23 us
  blocking collectives: 116 us -> 119 us
    pallas_call x0 -> x1, Pallas kernels: none -> 10.2 us  [part_scores(): pl.pallas_call(functools.partial(scores_kernel, quads, few), out_shape=ja...]
    dot_general x1 -> x0, matrix products: 4.98 us -> none  [product(): return lax.dot_general(left, right, NT, preferred_element_type=F32)]
    all_gather x1, blocking collectives: 33.7 us -> 36.1 us  [local(): out_rot = lax.all_gather(out_own, 'grp', axis=0, tiled=True)]
where the time goes in v3:
time: 195 us; the launch traced here: 194 us
  blocking collectives  119 us (61%)
  starting transfers between devices  45.1 us (23%)
  Pallas kernels  19.9 us (10%)
  local copies, waits for them, and re-layouts  5.56 us (3%)
  waiting for transfers between devices  3.27 us (2%)
    all_to_all x1, blocking collectives, local(): got = lax.all_to_all(sent, 'grp', 0, 0, axis_index_groups=alike)  43.4 us
    all_gather x1, blocking collectives, local(): out_rot = lax.all_gather(out_own, 'grp', axis=0, tiled=True)  36.1 us
    all_gather x1, blocking collectives, local(): lax.all_gather(acts, 'grp', axis=0, tiled=True, axis_index_groups=far)  24.2 us
    all_to_all x1, blocking collectives, local(): partial = lax.all_to_all(partial, 'shard', 0, 0, axis_index_groups=one_core)  14.8 us
    all_to_all x2, starting transfers between devices, spread(): return lax.all_to_all(copies, axis, 0, 0, axis_index_groups=groups)  14.1 us
    ppermute x3, starting transfers between devices, local(): lax.ppermute(basis_in, 'grp', [(to, to ^ at) for to in range(n_grp)])  10.5 us
    pallas_call x1, Pallas kernels, part_scores(): pl.pallas_call(functools.partial(scores_kernel, quads, few), out_shape=ja...  10.2 us
    all_to_all x1, starting transfers between devices, local(): lax.all_to_all(act_terms.reshape(n_shard, few, eig), 'shard', 0, 0)  7.49 us
  transfers between devices with their start and end apart: 11, of which 1 were waited for; matrix products, arithmetic and copies ran while one was open for 1% of the time, Pallas kernels for 4%

profile of v3, /device:TPU:32, one launch (start us, length us, event | category | flops | bytes accessed | tf_op | source)
XLA Modules:
  0.0 194.1 jit_solution(11711822624905476691)
XLA Ops:
  0.0 2.4 %broadcast_in_dim.6 = bf16[16,32,1728]{2,1,0:T(8,128)(2,1)} broadcast(bf16[32,1728]{1,0:T(8,128)(2,1)} %param.6), dimensions={1,2} | broadcast | bytes 1880064 | tf_op jit(solution)/shard_map/broadcast_in_dim | solution.py:21
  2.4 0.0 copy-start.3
  2.4 0.0 copy-start.5
  2.4 7.2 %all-to-all-start = ((bf16[16,32,1728]{2,1,0:T(8,128)(2,1)}), bf16[16,32,1728]{2,1,0:T(8,128)(2,1)S(1)}, u32[]{:S(2)}, u32[]{:S(2)}) async-start(bf16[16,32,1728]{2,1,0:T(8,128)(2,1)} %broadcast_in_dim.6), calls=%async_computation | async-start | bytes 3670016 | tf_op jit(solution)/shard_map/all_to_all | solution.py:22
  9.5 1.9 collective-permute-start
  11.5 0.0 copy-done.3
  11.5 3.8 %collective-permute-start.3 = (bf16[160,160]{1,0:T(8,128)(2,1)S(1)}, bf16[160,160]{1,0:T(8,128)(2,1)S(1)}, u32[]{:S(2)}, u32[]{:S(2)}) collective-permute-start(bf16[160,160]{1,0:T(8,128)(2,1)S(1)} %copy-done.3), channel_id=1, source_target_pairs={{0,96},{32,64},{64,32},{96,0},{128,224},{160,192},{192,160},{224,1... | collective-permute-start | bytes 153608 | tf_op jit(solution)/shard_map/ppermute | solution.py:211
  15.3 4.5 %collective-permute-start.4 = (bf16[160,160]{1,0:T(8,128)(2,1)S(1)}, bf16[160,160]{1,0:T(8,128)(2,1)S(1)}, u32[]{:S(2)}, u32[]{:S(2)}) collective-permute-start(bf16[160,160]{1,0:T(8,128)(2,1)S(1)} %copy-done.3), channel_id=1, source_target_pairs={{0,64},{32,96},{64,0},{96,32},{128,192},{160,224},{192,128},{224,1... | collective-permute-start | bytes 153608 | tf_op jit(solution)/shard_map/ppermute | solution.py:211
  19.8 2.2 %collective-permute-start.5 = (bf16[160,160]{1,0:T(8,128)(2,1)S(1)}, bf16[160,160]{1,0:T(8,128)(2,1)S(1)}, u32[]{:S(2)}, u32[]{:S(2)}) collective-permute-start(bf16[160,160]{1,0:T(8,128)(2,1)S(1)} %copy-done.3), channel_id=1, source_target_pairs={{0,32},{32,0},{64,96},{96,64},{128,160},{160,128},{192,224},{224,1... | collective-permute-start | bytes 153608 | tf_op jit(solution)/shard_map/ppermute | solution.py:211
  22.0 0.0 copy-done.5
  22.0 24.2 %all_gather.6 = bf16[256,160]{1,0:T(8,128)(2,1)S(1)} all-gather(bf16[64,160]{1,0:T(8,128)(2,1)S(1)} %bitcast.25), channel_id=1, replica_groups={{0,128,256,384},{32,160,288,416},{64,192,320,448},{96,224,352,480},{1,1..., dimensions={0}, use_global_device_ids=true | all-gather | bytes 102400 | tf_op jit(solution)/shard_map/all_gather | solution.py:218
  46.3 0.0 collective-permute-done.3
  46.3 0.0 collective-permute-done.4
  46.3 0.0 collective-permute-done.5
  46.3 1.2 convolution_bitcast_fusion
  47.5 0.0 all-to-all-done
  47.5 0.0 copy-start
  47.5 7.5 %all-to-all-start.1 = ((f32[32,8,640]{2,1,0:T(8,128)}), f32[32,8,640]{2,1,0:T(8,128)S(1)}, u32[]{:S(2)}, u32[]{:S(2)}) async-start(f32[32,8,640]{2,1,0:T(8,128)} %convolution_bitcast_fusion), calls=%async_computation.1 | async-start | bytes 1310720 | tf_op jit(solution)/shard_map/all_to_all | solution.py:220
  55.0 0.0 collective-permute-done.other_hbm
  55.1 0.0 copy-done
  55.1 7.5 %out_terms.1 = (f32[8,32,864]{2,1,0:T(8,128)}, bf16[8,32,512]{2,1,0:T(8,128)(2,1)}, bf16[8,32,352]{2,1,0:T(8,128)(2,1)}) custom-call(s32[1]{0:T(128)} %bitcast.parity_ref, bf16[512,1728]{1,0:T(8,128)(2,1)} %bitcast.21, bf16[432,1728]{1,0:T(8,128)(2,1)} %bitcast.30, bf16[432,1728]{1,0:T(8,128)(2,1)} %collective-permute-done.other_hbm), custom_call_target="tpu_custom_call" | custom-call | flops 1528823808 | bytes 6291456 | tf_op jit(solution)/shard_map/out_terms/pallas_call | solution.py:63
  62.5 3.6 %collective-permute-start.1 = (bf16[8,32,512]{2,1,0:T(8,128)(2,1)}, bf16[8,32,512]{2,1,0:T(8,128)(2,1)S(1)}, u32[]{:S(2)}, u32[]{:S(2)}) collective-permute-start(bf16[8,32,512]{2,1,0:T(8,128)(2,1)} %get-tuple-element.9), channel_id=1, source_target_pairs={{0,32},{32,0},{64,96},{96,64},{128,160},{160,128},{192,224},{224,1... | collective-permute-start | bytes 786440 | tf_op jit(solution)/shard_map/ppermute | solution.py:226
  66.2 3.2 %collective-permute-start.2 = (bf16[8,32,352]{2,1,0:T(8,128)(2,1)}, bf16[8,32,352]{2,1,0:T(8,128)(2,1)S(1)}, u32[]{:S(2)}, u32[]{:S(2)}) collective-permute-start(bf16[8,32,352]{2,1,0:T(8,128)(2,1)} %get-tuple-element.10), channel_id=1, source_target_pairs={{0,480},{32,64},{64,32},{96,128},{128,96},{160,192},{192,160},{224... | collective-permute-start | bytes 540680 | tf_op jit(solution)/shard_map/ppermute | solution.py:227
  69.4 0.0 all-to-all-done.1
  69.4 0.1 reduce_sum.30.own_ref
  69.5 0.0 copy-start.4
  69.5 2.4 %collective-permute-start.6 = (bf16[8,640]{1,0:T(8,128)(2,1)S(1)}, bf16[8,640]{1,0:T(8,128)(2,1)S(1)}, u32[]{:S(2)}, u32[]{:S(2)}) collective-permute-start(bf16[8,640]{1,0:T(8,128)(2,1)S(1)} %reduce_sum.30.own_ref), channel_id=1, source_target_pairs={{0,32},{32,0},{64,96},{96,64},{128,160},{160,128},{192,224},{224,1... | collective-permute-start | bytes 30728 | tf_op jit(solution)/shard_map/ppermute | solution.py:222
  71.8 3.2 %collective-permute-done.6.near_ref = bf16[8,640]{1,0:T(8,128)(2,1)S(1)} collective-permute-done((bf16[8,640]{1,0:T(8,128)(2,1)S(1)}, bf16[8,640]{1,0:T(8,128)(2,1)S(1)}, u32[]{:S(2)}, u32[]{:S(2)}) %collective-permute-start.6) | collective-permute-done | bytes 10272 | tf_op jit(solution)/shard_map/ppermute | solution.py:222
  75.0 0.0 copy-start.6
  75.0 0.0 collective-permute-done.2.high_ref
  75.1 0.0 copy-start.2
  75.1 0.0 collective-permute-done.1.low_ref
  75.1 0.0 copy-start.1
  75.1 0.0 copy-done.4
  75.1 0.5 copy-done.6
  75.6 0.1 copy-done.2
  75.8 0.1 copy-done.1
  75.9 2.2 %message.1 = bf16[8,32,1248]{2,1,0:T(8,128)(2,1)} custom-call(s32[1]{0:T(128)} %bitcast.parity_ref, f32[8,32,864]{2,1,0:T(8,128)} %get-tuple-element.8.keep_ref, bf16[8,32,512]{2,1,0:T(8,128)(2,1)} %copy-done.1, bf16[8,32,352]{2,1,0:T(8,128)(2,1)} %copy-done.2, bf16[8,640]{1,0:T(8,128)(2,1)} %copy-done.4, bf16[8,640]{1,0:T(8,128)(2,1)} %copy-done.6), custom_call_target="tpu_custom_call" | custom-call | flops 1048576 | bytes 2097152 | tf_op jit(solution)/shard_map/message/pallas_call | solution.py:100
  78.1 43.4 %all_to_all.25 = bf16[8,32,1248]{2,1,0:T(8,128)(2,1)S(1)} all-to-all(bf16[8,32,1248]{2,1,0:T(8,128)(2,1)} %message.1), channel_id=1, replica_groups={{0,64,128,192,256,320,384,448},{32,96,160,224,288,352,416,480},{1,65,12..., dimensions={0} | all-to-all | bytes 1277952 | tf_op jit(solution)/shard_map/all_to_all | solution.py:232
  121.6 0.1 copy.8
  121.7 1.8 broadcast_in_dim.15
  123.5 0.0 copy-start.7
  123.5 6.9 %all-to-all-start.3 = ((bf16[16,32,2560]{2,1,0:T(8,128)(2,1)}), bf16[16,32,2560]{2,1,0:T(8,128)(2,1)}, u32[]{:S(2)}, u32[]{:S(2)}) async-start(bf16[16,32,2560]{2,1,0:T(8,128)(2,1)} %broadcast_in_dim.15), calls=%async_computation.3 | async-start | bytes 5242880 | tf_op jit(solution)/shard_map/all_to_all | solution.py:22
  130.4 0.0 copy-done.7
  130.4 1.9 collective-permute-start.7
  132.4 0.1 slice_reduce_fusion
  132.4 36.1 %all_gather.7.out_hbm = bf16[512,864]{1,0:T(8,128)(2,1)} all-gather(bf16[32,864]{1,0:T(8,128)(2,1)S(1)} %slice_reduce_fusion), channel_id=1, replica_groups=mesh['grp'=16,'shard'=32] {'grp'}, dimensions={0}, use_global_device_ids=true | all-gather | bytes 940032 | tf_op jit(solution)/shard_map/all_gather | solution.py:238
  168.5 0.0 collective-permute-done.7.other_hbm
  168.5 0.0 all-to-all-done.3
  168.5 10.2 %part_scores.1 = f32[16,8,128]{2,1,0:T(8,128)} custom-call(bf16[512,2560]{1,0:T(8,128)(2,1)} %bitcast.10.act_hbm, bf16[432,2560]{1,0:T(8,128)(2,1)} %bitcast.27, bf16[432,2560]{1,0:T(8,128)(2,1)} %collective-permute-done.7.other_hbm, bf16[512,864]{1,0:T(8,128)(2,1)} %all_gather.7.out_hbm), custom_call_target="tpu_custom_call" | custom-call | flops 2264924160 | bytes 8388608 | tf_op jit(solution)/shard_map/part_scores/pallas_call | solution.py:168
  178.8 14.8 %all_to_all.26 = f32[16,8,128]{2,1,0:T(8,128)S(1)} all-to-all(f32[16,8,128]{2,1,0:T(8,128)} %part_scores.1), channel_id=1, replica_groups={{0,2,4,6,8,10,12,14,16,18,20,22,24,26,28,30},{1,3,5,7,9,11,13,15,17,19,..., dimensions={0} | all-to-all | bytes 131072 | tf_op jit(solution)/shard_map/all_to_all | solution.py:241
  193.6 0.5 slice.15
  (7 shorter events, 0.1 us)
Async XLA Ops:
  2.4 9.1 %copy-start.3 = (bf16[160,160]{1,0:T(8,128)(2,1)S(1)}, bf16[160,160]{1,0:T(8,128)(2,1)}, u32[]{:S(2)}) copy-start(bf16[160,160]{1,0:T(8,128)(2,1)} %param.7) | copy-start | bytes 153604
  2.4 19.6 %copy-start.5 = (bf16[64,160]{1,0:T(8,128)(2,1)S(1)}, bf16[64,160]{1,0:T(8,128)(2,1)}, u32[]{:S(2)}) copy-start(bf16[64,160]{1,0:T(8,128)(2,1)} %param.5) | copy-start | bytes 61444
  2.4 45.2 %all-to-all-start = ((bf16[16,32,1728]{2,1,0:T(8,128)(2,1)}), bf16[16,32,1728]{2,1,0:T(8,128)(2,1)S(1)}, u32[]{:S(2)}, u32[]{:S(2)}) async-start(bf16[16,32,1728]{2,1,0:T(8,128)(2,1)} %broadcast_in_dim.6), calls=%async_computation | async-start | bytes 3670016 | tf_op jit(solution)/shard_map/all_to_all | solution.py:22
  9.5 45.5 %collective-permute-start = (bf16[432,1728]{1,0:T(8,128)(2,1)}, bf16[432,1728]{1,0:T(8,128)(2,1)}, u32[]{:S(2)}, u32[]{:S(2)}) collective-permute-start(bf16[432,1728]{1,0:T(8,128)(2,1)} %bitcast.29), channel_id=1, source_target_pairs={{0,1},{1,0},{2,3},{3,2},{4,5},{5,4},{6,7},{7,6},{8,9},{9,8},{10,11... | collective-permute-start | bytes 4478984 | tf_op jit(solution)/shard_map/ppermute | solution.py:205
  11.5 34.8 %collective-permute-start.3 = (bf16[160,160]{1,0:T(8,128)(2,1)S(1)}, bf16[160,160]{1,0:T(8,128)(2,1)S(1)}, u32[]{:S(2)}, u32[]{:S(2)}) collective-permute-start(bf16[160,160]{1,0:T(8,128)(2,1)S(1)} %copy-done.3), channel_id=1, source_target_pairs={{0,96},{32,64},{64,32},{96,0},{128,224},{160,192},{192,160},{224,1... | collective-permute-start | bytes 153608 | tf_op jit(solution)/shard_map/ppermute | solution.py:211
  15.3 30.9 %collective-permute-start.4 = (bf16[160,160]{1,0:T(8,128)(2,1)S(1)}, bf16[160,160]{1,0:T(8,128)(2,1)S(1)}, u32[]{:S(2)}, u32[]{:S(2)}) collective-permute-start(bf16[160,160]{1,0:T(8,128)(2,1)S(1)} %copy-done.3), channel_id=1, source_target_pairs={{0,64},{32,96},{64,0},{96,32},{128,192},{160,224},{192,128},{224,1... | collective-permute-start | bytes 153608 | tf_op jit(solution)/shard_map/ppermute | solution.py:211
  19.8 26.5 %collective-permute-start.5 = (bf16[160,160]{1,0:T(8,128)(2,1)S(1)}, bf16[160,160]{1,0:T(8,128)(2,1)S(1)}, u32[]{:S(2)}, u32[]{:S(2)}) collective-permute-start(bf16[160,160]{1,0:T(8,128)(2,1)S(1)} %copy-done.3), channel_id=1, source_target_pairs={{0,32},{32,0},{64,96},{96,64},{128,160},{160,128},{192,224},{224,1... | collective-permute-start | bytes 153608 | tf_op jit(solution)/shard_map/ppermute | solution.py:211
  47.5 7.5 %copy-start = (bf16[16,32,1728]{2,1,0:T(8,128)(2,1)}, bf16[16,32,1728]{2,1,0:T(8,128)(2,1)S(1)}, u32[]{:S(2)}) copy-start(bf16[16,32,1728]{2,1,0:T(8,128)(2,1)S(1)} %all-to-all-done) | copy-start | bytes 5308420
  47.5 21.9 %all-to-all-start.1 = ((f32[32,8,640]{2,1,0:T(8,128)}), f32[32,8,640]{2,1,0:T(8,128)S(1)}, u32[]{:S(2)}, u32[]{:S(2)}) async-start(f32[32,8,640]{2,1,0:T(8,128)} %convolution_bitcast_fusion), calls=%async_computation.1 | async-start | bytes 1310720 | tf_op jit(solution)/shard_map/all_to_all | solution.py:220
  62.5 12.6 %collective-permute-start.1 = (bf16[8,32,512]{2,1,0:T(8,128)(2,1)}, bf16[8,32,512]{2,1,0:T(8,128)(2,1)S(1)}, u32[]{:S(2)}, u32[]{:S(2)}) collective-permute-start(bf16[8,32,512]{2,1,0:T(8,128)(2,1)} %get-tuple-element.9), channel_id=1, source_target_pairs={{0,32},{32,0},{64,96},{96,64},{128,160},{160,128},{192,224},{224,1... | collective-permute-start | bytes 786440 | tf_op jit(solution)/shard_map/ppermute | solution.py:226
  66.2 8.9 %collective-permute-start.2 = (bf16[8,32,352]{2,1,0:T(8,128)(2,1)}, bf16[8,32,352]{2,1,0:T(8,128)(2,1)S(1)}, u32[]{:S(2)}, u32[]{:S(2)}) collective-permute-start(bf16[8,32,352]{2,1,0:T(8,128)(2,1)} %get-tuple-element.10), channel_id=1, source_target_pairs={{0,480},{32,64},{64,32},{96,128},{128,96},{160,192},{192,160},{224... | collective-permute-start | bytes 540680 | tf_op jit(solution)/shard_map/ppermute | solution.py:227
  69.5 5.6 %copy-start.4 = (bf16[8,640]{1,0:T(8,128)(2,1)}, bf16[8,640]{1,0:T(8,128)(2,1)S(1)}, u32[]{:S(2)}) copy-start(bf16[8,640]{1,0:T(8,128)(2,1)S(1)} %reduce_sum.30.own_ref) | copy-start | bytes 30724
  69.5 5.6 %collective-permute-start.6 = (bf16[8,640]{1,0:T(8,128)(2,1)S(1)}, bf16[8,640]{1,0:T(8,128)(2,1)S(1)}, u32[]{:S(2)}, u32[]{:S(2)}) collective-permute-start(bf16[8,640]{1,0:T(8,128)(2,1)S(1)} %reduce_sum.30.own_ref), channel_id=1, source_target_pairs={{0,32},{32,0},{64,96},{96,64},{128,160},{160,128},{192,224},{224,1... | collective-permute-start | bytes 30728 | tf_op jit(solution)/shard_map/ppermute | solution.py:222
  75.0 0.6 copy-start.6
  75.1 0.7 copy-start.2
  75.1 0.8 copy-start.1
  123.5 6.9 %copy-start.7 = (bf16[1,2560,432]{1,2,0:T(8,128)(2,1)S(1)}, bf16[1,2560,432]{1,2,0:T(8,128)(2,1)}, u32[]{:S(2)}) copy-start(bf16[1,2560,432]{1,2,0:T(8,128)(2,1)} %param.9) | copy-start | bytes 6635524
  123.5 45.0 %all-to-all-start.3 = ((bf16[16,32,2560]{2,1,0:T(8,128)(2,1)}), bf16[16,32,2560]{2,1,0:T(8,128)(2,1)}, u32[]{:S(2)}, u32[]{:S(2)}) async-start(bf16[16,32,2560]{2,1,0:T(8,128)(2,1)} %broadcast_in_dim.15), calls=%async_computation.3 | async-start | bytes 5242880 | tf_op jit(solution)/shard_map/all_to_all | solution.py:22
  130.4 38.1 %collective-permute-start.7 = (bf16[432,2560]{1,0:T(8,128)(2,1)S(1)}, bf16[432,2560]{1,0:T(8,128)(2,1)}, u32[]{:S(2)}, u32[]{:S(2)}) collective-permute-start(bf16[432,2560]{1,0:T(8,128)(2,1)S(1)} %bitcast.28), channel_id=1, source_target_pairs={{0,1},{1,0},{2,3},{3,2},{4,5},{5,4},{6,7},{7,6},{8,9},{9,8},{10,11... | collective-permute-start | bytes 6635528 | tf_op jit(solution)/shard_map/ppermute | solution.py:207

commit v4 on v2

--- a/solution.py
+++ b/solution.py
@@ -79,21 +79,23 @@
     odd = parity_ref[0] == 1
     own, near = own_ref[...].astype(F32), near_ref[...].astype(F32)
     act = jnp.concatenate([jnp.where(odd, near, own), jnp.where(odd, own, near)], axis=0)
-    rest = act[:, wide:]
-    blank = jnp.zeros((act.shape[0], 2 * wide - act.shape[1]), F32)
-    act = jnp.concatenate([act[:, :wide], jnp.concatenate([rest, blank], axis=1)], axis=0)
     act = act.astype(BF16)
+    rows, cols = act.shape[0], keep_ref.shape[2]
+    blank = jnp.zeros((rows, wide - cols), BF16)
     for block in range(keep_ref.shape[0]):
-        sent_ref[block, :, :wide] = act
-        low = keep_ref[block, :, :CUT] + low_ref[block].astype(F32)
-        sent_ref[block, :, wide : wide + CUT] = low.astype(BF16)
-        high = keep_ref[block, :, CUT:] + high_ref[block].astype(F32)
-        sent_ref[block, :, wide + CUT :] = high.astype(BF16)
+        low = (keep_ref[block, :, :CUT] + low_ref[block].astype(F32)).astype(BF16)
+        high = (keep_ref[block, :, CUT:] + high_ref[block].astype(F32)).astype(BF16)
+        for at in range(2):
+            begin, part = at * wide, slice(at * rows, (at + 1) * rows)
+            sent_ref[block, :, begin : begin + CUT] = low[part]
+            sent_ref[block, :, begin + CUT : begin + cols] = high[part]
+            sent_ref[block, :, begin + cols : begin + wide] = blank
+        sent_ref[block, :, 2 * wide :] = act
 
 
 def message(parity, keep, low, high, own, near, wide):
     smem, vmem = pl.BlockSpec(memory_space=pltpu.SMEM), pl.BlockSpec(memory_space=pltpu.VMEM)
-    shape = (*keep.shape[:2], wide + keep.shape[2])
+    shape = (keep.shape[0], keep.shape[1] // 2, 2 * wide + own.shape[1])
     return pl.pallas_call(
         functools.partial(message_kernel, wide),
         out_shape=jax.ShapeDtypeStruct(shape, BF16),
@@ -102,6 +104,27 @@
         cost_estimate=pl.CostEstimate(flops=1 << 20, bytes_accessed=2 << 20, transcendentals=0),
         name="message",
     )(parity, keep, low, high, own, near)
+
+
+def own_kernel(wide, got_ref, out_ref):
+    rows, cols = got_ref.shape[1], out_ref.shape[1]
+    for at in range(2):
+        total = jnp.zeros((rows, cols), F32)
+        for block in range(got_ref.shape[0]):
+            total = total + got_ref[block, :, at * wide : at * wide + cols].astype(F32)
+        out_ref[at * rows : (at + 1) * rows] = total.astype(BF16)
+
+
+def own_terms(got, cols, wide):
+    vmem = pl.BlockSpec(memory_space=pltpu.VMEM)
+    return pl.pallas_call(
+        functools.partial(own_kernel, wide),
+        out_shape=jax.ShapeDtypeStruct((2 * got.shape[1], cols), BF16),
+        in_specs=[vmem],
+        out_specs=vmem,
+        cost_estimate=pl.CostEstimate(flops=1 << 18, bytes_accessed=1 << 19, transcendentals=0),
+        name="own_terms",
+    )(got)
 
 
 def local(activations, grad_outputs, basis_in, basis_out, query_grads):
@@ -148,12 +171,12 @@
     low = lax.ppermute(low, "grp", pairs)
     high = lax.ppermute(high, "grp", cross_pairs)
 
-    wide = -(-eig // 256) * 128
-    skip = 2 * wide - eig
+    cols = keep.shape[2]
+    wide = -(-cols // 128) * 128
     sent = message(parity_at, keep, low, high, act_own, act_near, wide)
     got = lax.all_to_all(sent, "grp", 0, 0, axis_index_groups=alike)
-    out_own = jnp.sum(got[:, :, wide:].astype(F32), axis=0).astype(BF16)
-    act_rot = jnp.concatenate([got[:, : 2 * few, :wide], got[:, 2 * few :, : wide - skip]], axis=2)
+    out_own = own_terms(got, cols, wide)
+    act_rot = got[:, :, 2 * wide :]
     act_rot = act_rot.reshape(quads, 2, 2 * few, eig).transpose(1, 2, 0, 3)
     act_rot = act_rot.reshape(rows, quads * eig)
     act_rot = spread(act_rot, "shard", chips, one_core).reshape(half, quads * eig)

time: 188 us -> 190 us (1.011)
    all_gather x1, blocking collectives: 33.7 us -> 35.8 us  [local(): out_rot = lax.all_gather(out_own, 'grp', axis=0, tiled=True)]
where the time goes in v4:
time: 190 us; the launch traced here: 189 us
  blocking collectives  117 us (62%)
  starting transfers between devices  45.8 us (24%)
  Pallas kernels  10.6 us (6%)
  matrix products  6.73 us (4%)
  local copies, waits for them, and re-layouts  5.75 us (3%)
  waiting for transfers between devices  2.44 us (1%)
    all_to_all x1, blocking collectives, local(): got = lax.all_to_all(sent, 'grp', 0, 0, axis_index_groups=alike)  42.4 us
    all_gather x1, blocking collectives, local(): out_rot = lax.all_gather(out_own, 'grp', axis=0, tiled=True)  35.8 us
    all_gather x1, blocking collectives, local(): lax.all_gather(acts, 'grp', axis=0, tiled=True, axis_index_groups=far)  24.2 us
    all_to_all x1, blocking collectives, local(): partial = lax.all_to_all(partial, 'shard', 0, 0, axis_index_groups=one_core)  14.7 us
    all_to_all x2, starting transfers between devices, spread(): return lax.all_to_all(copies, axis, 0, 0, axis_index_groups=groups)  14 us
    ppermute x3, starting transfers between devices, local(): lax.ppermute(basis_in, 'grp', [(to, to ^ at) for to in range(n_grp)])  10.5 us
    all_to_all x1, starting transfers between devices, local(): lax.all_to_all(act_terms.reshape(n_shard, few, eig), 'shard', 0, 0)  7.49 us
    pallas_call x1, Pallas kernels, out_terms(): pl.pallas_call(functools.partial(terms_kernel, quads, few), out_shape=(ja...  6.63 us
  transfers between devices with their start and end apart: 11, of which 1 were waited for; matrix products, arithmetic and copies ran while one was open for 1% of the time, Pallas kernels for 4%

profile of v4, /device:TPU:32, one launch (start us, length us, event | category | flops | bytes accessed | tf_op | source)
XLA Modules:
  0.0 188.8 jit_solution(4871196089949740388)
XLA Ops:
  0.0 2.4 %broadcast_in_dim.6 = bf16[16,32,1728]{2,1,0:T(8,128)(2,1)} broadcast(bf16[32,1728]{1,0:T(8,128)(2,1)} %param.6), dimensions={1,2} | broadcast | bytes 1880064 | tf_op jit(solution)/shard_map/broadcast_in_dim | solution.py:21
  2.4 0.0 copy-start.4
  2.4 0.0 copy-start.6
  2.4 7.2 %all-to-all-start = ((bf16[16,32,1728]{2,1,0:T(8,128)(2,1)}), bf16[16,32,1728]{2,1,0:T(8,128)(2,1)S(1)}, u32[]{:S(2)}, u32[]{:S(2)}) async-start(bf16[16,32,1728]{2,1,0:T(8,128)(2,1)} %broadcast_in_dim.6), calls=%async_computation | async-start | bytes 3670016 | tf_op jit(solution)/shard_map/all_to_all | solution.py:22
  9.5 1.9 %collective-permute-start = (bf16[432,1728]{1,0:T(8,128)(2,1)}, bf16[432,1728]{1,0:T(8,128)(2,1)}, u32[]{:S(2)}, u32[]{:S(2)}) collective-permute-start(bf16[432,1728]{1,0:T(8,128)(2,1)} %bitcast.35), channel_id=1, source_target_pairs={{0,1},{1,0},{2,3},{3,2},{4,5},{5,4},{6,7},{7,6},{8,9},{9,8},{10,11... | collective-permute-start | bytes 4478984 | tf_op jit(solution)/shard_map/ppermute | solution.py:150
  11.5 0.0 copy-done.4
  11.5 3.8 %collective-permute-start.3 = (bf16[160,160]{1,0:T(8,128)(2,1)S(1)}, bf16[160,160]{1,0:T(8,128)(2,1)S(1)}, u32[]{:S(2)}, u32[]{:S(2)}) collective-permute-start(bf16[160,160]{1,0:T(8,128)(2,1)S(1)} %copy-done.4), channel_id=1, source_target_pairs={{0,96},{32,64},{64,32},{96,0},{128,224},{160,192},{192,160},{224,1... | collective-permute-start | bytes 153608 | tf_op jit(solution)/shard_map/ppermute | solution.py:156
  15.3 4.5 %collective-permute-start.4 = (bf16[160,160]{1,0:T(8,128)(2,1)S(1)}, bf16[160,160]{1,0:T(8,128)(2,1)S(1)}, u32[]{:S(2)}, u32[]{:S(2)}) collective-permute-start(bf16[160,160]{1,0:T(8,128)(2,1)S(1)} %copy-done.4), channel_id=1, source_target_pairs={{0,64},{32,96},{64,0},{96,32},{128,192},{160,224},{192,128},{224,1... | collective-permute-start | bytes 153608 | tf_op jit(solution)/shard_map/ppermute | solution.py:156
  19.8 2.2 %collective-permute-start.5 = (bf16[160,160]{1,0:T(8,128)(2,1)S(1)}, bf16[160,160]{1,0:T(8,128)(2,1)S(1)}, u32[]{:S(2)}, u32[]{:S(2)}) collective-permute-start(bf16[160,160]{1,0:T(8,128)(2,1)S(1)} %copy-done.4), channel_id=1, source_target_pairs={{0,32},{32,0},{64,96},{96,64},{128,160},{160,128},{192,224},{224,1... | collective-permute-start | bytes 153608 | tf_op jit(solution)/shard_map/ppermute | solution.py:156
  22.0 0.0 copy-done.6
  22.0 24.2 %all_gather.6 = bf16[256,160]{1,0:T(8,128)(2,1)S(1)} all-gather(bf16[64,160]{1,0:T(8,128)(2,1)S(1)} %bitcast.29), channel_id=1, replica_groups={{0,128,256,384},{32,160,288,416},{64,192,320,448},{96,224,352,480},{1,1..., dimensions={0}, use_global_device_ids=true | all-gather | bytes 102400 | tf_op jit(solution)/shard_map/all_gather | solution.py:163
  46.3 0.0 collective-permute-done.3
  46.3 0.0 collective-permute-done.4
  46.3 0.0 collective-permute-done.5
  46.3 1.2 convolution_bitcast_fusion
  47.5 0.0 all-to-all-done
  47.5 0.0 copy-start.1
  47.5 7.5 %all-to-all-start.1 = ((f32[32,8,640]{2,1,0:T(8,128)}), f32[32,8,640]{2,1,0:T(8,128)S(1)}, u32[]{:S(2)}, u32[]{:S(2)}) async-start(f32[32,8,640]{2,1,0:T(8,128)} %convolution_bitcast_fusion), calls=%async_computation.1 | async-start | bytes 1310720 | tf_op jit(solution)/shard_map/all_to_all | solution.py:165
  55.0 0.0 collective-permute-done.other_hbm
  55.1 0.0 copy-done.1
  55.1 6.6 %out_terms.1 = (f32[8,32,864]{2,1,0:T(8,128)}, bf16[8,32,512]{2,1,0:T(8,128)(2,1)}, bf16[8,32,352]{2,1,0:T(8,128)(2,1)}) custom-call(s32[1]{0:T(128)} %bitcast.parity_ref, bf16[512,1728]{1,0:T(8,128)(2,1)} %bitcast.25, bf16[432,1728]{1,0:T(8,128)(2,1)} %bitcast.36, bf16[432,1728]{1,0:T(8,128)(2,1)} %collective-permute-done.other_hbm), custom_call_target="tpu_custom_call" | custom-call | flops 1528823808 | bytes 6291456 | tf_op jit(solution)/shard_map/out_terms/pallas_call | solution.py:59
  61.7 3.6 %collective-permute-start.1 = (bf16[8,32,512]{2,1,0:T(8,128)(2,1)}, bf16[8,32,512]{2,1,0:T(8,128)(2,1)S(1)}, u32[]{:S(2)}, u32[]{:S(2)}) collective-permute-start(bf16[8,32,512]{2,1,0:T(8,128)(2,1)} %get-tuple-element.9), channel_id=1, source_target_pairs={{0,32},{32,0},{64,96},{96,64},{128,160},{160,128},{192,224},{224,1... | collective-permute-start | bytes 786440 | tf_op jit(solution)/shard_map/ppermute | solution.py:171
  65.4 3.2 %collective-permute-start.2 = (bf16[8,32,352]{2,1,0:T(8,128)(2,1)}, bf16[8,32,352]{2,1,0:T(8,128)(2,1)S(1)}, u32[]{:S(2)}, u32[]{:S(2)}) collective-permute-start(bf16[8,32,352]{2,1,0:T(8,128)(2,1)} %get-tuple-element.10), channel_id=1, source_target_pairs={{0,480},{32,64},{64,32},{96,128},{128,96},{160,192},{192,160},{224... | collective-permute-start | bytes 540680 | tf_op jit(solution)/shard_map/ppermute | solution.py:172
  68.6 0.0 all-to-all-done.1
  68.6 0.1 reduce_sum.27.own_ref
  68.6 0.0 copy-start.5
  68.6 3.2 %collective-permute-start.6 = (bf16[8,640]{1,0:T(8,128)(2,1)S(1)}, bf16[8,640]{1,0:T(8,128)(2,1)S(1)}, u32[]{:S(2)}, u32[]{:S(2)}) collective-permute-start(bf16[8,640]{1,0:T(8,128)(2,1)S(1)} %reduce_sum.27.own_ref), channel_id=1, source_target_pairs={{0,32},{32,0},{64,96},{96,64},{128,160},{160,128},{192,224},{224,1... | collective-permute-start | bytes 30728 | tf_op jit(solution)/shard_map/ppermute | solution.py:167
  71.8 2.4 %collective-permute-done.6.near_ref = bf16[8,640]{1,0:T(8,128)(2,1)S(1)} collective-permute-done((bf16[8,640]{1,0:T(8,128)(2,1)S(1)}, bf16[8,640]{1,0:T(8,128)(2,1)S(1)}, u32[]{:S(2)}, u32[]{:S(2)}) %collective-permute-start.6) | collective-permute-done | bytes 10272 | tf_op jit(solution)/shard_map/ppermute | solution.py:167
  74.2 0.0 copy-start.7
  74.2 0.0 collective-permute-done.2.high_ref
  74.3 0.0 copy-start.3
  74.3 0.0 collective-permute-done.1.low_ref
  74.3 0.0 copy-start.2
  74.3 0.0 copy-done.5
  74.3 0.5 copy-done.7
  74.8 0.1 copy-done.3
  74.9 0.1 copy-done.2
  75.0 2.2 %message.1 = bf16[8,16,2432]{2,1,0:T(8,128)(2,1)} custom-call(s32[1]{0:T(128)} %bitcast.parity_ref, f32[8,32,864]{2,1,0:T(8,128)} %get-tuple-element.8.keep_ref, bf16[8,32,512]{2,1,0:T(8,128)(2,1)} %copy-done.2, bf16[8,32,352]{2,1,0:T(8,128)(2,1)} %copy-done.3, bf16[8,640]{1,0:T(8,128)(2,1)} %copy-done.5, bf16[8,640]{1,0:T(8,128)(2,1)} %copy-done.7), custom_call_target="tpu_custom_call" | custom-call | flops 1048576 | bytes 2097152 | tf_op jit(solution)/shard_map/message/pallas_call | solution.py:99
  77.3 42.4 %all_to_all.25.got_ref = bf16[8,16,2432]{2,1,0:T(8,128)(2,1)S(1)} all-to-all(bf16[8,16,2432]{2,1,0:T(8,128)(2,1)} %message.1), channel_id=1, replica_groups={{0,64,128,192,256,320,384,448},{32,96,160,224,288,352,416,480},{1,65,12..., dimensions={0} | all-to-all | bytes 1245184 | tf_op jit(solution)/shard_map/all_to_all | solution.py:177
  119.7 0.0 copy-start
  119.7 0.1 copy.14
  119.8 1.8 broadcast_in_dim.15
  121.6 0.0 copy-done
  121.6 6.8 %all-to-all-start.3 = ((bf16[16,32,2560]{2,1,0:T(8,128)(2,1)}), bf16[16,32,2560]{2,1,0:T(8,128)(2,1)S(1)}, u32[]{:S(2)}, u32[]{:S(2)}) async-start(bf16[16,32,2560]{2,1,0:T(8,128)(2,1)} %broadcast_in_dim.15), calls=%async_computation.3 | async-start | bytes 5242880 | tf_op jit(solution)/shard_map/all_to_all | solution.py:22
  128.4 1.9 %collective-permute-start.7 = (bf16[432,2560]{1,0:T(8,128)(2,1)}, bf16[432,2560]{1,0:T(8,128)(2,1)}, u32[]{:S(2)}, u32[]{:S(2)}) collective-permute-start(bf16[432,2560]{1,0:T(8,128)(2,1)} %bitcast.33), channel_id=1, source_target_pairs={{0,1},{1,0},{2,3},{3,2},{4,5},{5,4},{6,7},{7,6},{8,9},{9,8},{10,11... | collective-permute-start | bytes 6635528 | tf_op jit(solution)/shard_map/ppermute | solution.py:152
  130.3 1.8 own_terms.1
  132.1 35.8 %all_gather.7 = bf16[512,864]{1,0:T(8,128)(2,1)} all-gather(bf16[32,864]{1,0:T(8,128)(2,1)} %own_terms.1), channel_id=1, replica_groups=mesh['grp'=16,'shard'=32] {'grp'}, dimensions={0}, use_global_device_ids=true | all-gather | bytes 940032 | tf_op jit(solution)/shard_map/all_gather | solution.py:183
  167.9 0.0 collective-permute-done.7
  167.9 0.0 all-to-all-done.3
  167.9 5.5 %multiply_reduce_fusion = f32[512]{0:T(512)S(1)} fusion(bf16[512,864]{1,0:T(8,128)(2,1)} %all_gather.7, bf16[512,2560]{1,0:T(8,128)(2,1)S(1)} %bitcast.24, bf16[432,2560]{1,0:T(8,128)(2,1)} %collective-permute-done.7, bf16[432,2560]{1,0:T(8,128)(2,1)} %bitcast.34), kind=kOutput, calls=%fused_computation.4 | convolution fusion | flops 2275098112 | bytes 7931904 | tf_op jit(solution)/shard_map/dot_general | solution.py:17
  173.4 0.1 reshape.36
  173.5 0.1 reshape.37
  173.6 14.7 %all_to_all.26 = f32[16,8,128]{2,1,0:T(8,128)S(1)} all-to-all(f32[16,8,128]{2,1,0:T(8,128)S(1)} %pad.4.clone), channel_id=1, replica_groups={{0,2,4,6,8,10,12,14,16,18,20,22,24,26,28,30},{1,3,5,7,9,11,13,15,17,19,..., dimensions={0} | all-to-all | bytes 131072 | tf_op jit(solution)/shard_map/all_to_all | solution.py:189
  188.3 0.5 slice.7
  (7 shorter events, 0.1 us)
Async XLA Ops:
  2.4 9.1 %copy-start.4 = (bf16[160,160]{1,0:T(8,128)(2,1)S(1)}, bf16[160,160]{1,0:T(8,128)(2,1)}, u32[]{:S(2)}) copy-start(bf16[160,160]{1,0:T(8,128)(2,1)} %param.7) | copy-start | bytes 153604
  2.4 19.6 %copy-start.6 = (bf16[64,160]{1,0:T(8,128)(2,1)S(1)}, bf16[64,160]{1,0:T(8,128)(2,1)}, u32[]{:S(2)}) copy-start(bf16[64,160]{1,0:T(8,128)(2,1)} %param.5) | copy-start | bytes 61444
  2.4 45.2 %all-to-all-start = ((bf16[16,32,1728]{2,1,0:T(8,128)(2,1)}), bf16[16,32,1728]{2,1,0:T(8,128)(2,1)S(1)}, u32[]{:S(2)}, u32[]{:S(2)}) async-start(bf16[16,32,1728]{2,1,0:T(8,128)(2,1)} %broadcast_in_dim.6), calls=%async_computation | async-start | bytes 3670016 | tf_op jit(solution)/shard_map/all_to_all | solution.py:22
  9.5 45.5 %collective-permute-start = (bf16[432,1728]{1,0:T(8,128)(2,1)}, bf16[432,1728]{1,0:T(8,128)(2,1)}, u32[]{:S(2)}, u32[]{:S(2)}) collective-permute-start(bf16[432,1728]{1,0:T(8,128)(2,1)} %bitcast.35), channel_id=1, source_target_pairs={{0,1},{1,0},{2,3},{3,2},{4,5},{5,4},{6,7},{7,6},{8,9},{9,8},{10,11... | collective-permute-start | bytes 4478984 | tf_op jit(solution)/shard_map/ppermute | solution.py:150
  11.5 34.8 %collective-permute-start.3 = (bf16[160,160]{1,0:T(8,128)(2,1)S(1)}, bf16[160,160]{1,0:T(8,128)(2,1)S(1)}, u32[]{:S(2)}, u32[]{:S(2)}) collective-permute-start(bf16[160,160]{1,0:T(8,128)(2,1)S(1)} %copy-done.4), channel_id=1, source_target_pairs={{0,96},{32,64},{64,32},{96,0},{128,224},{160,192},{192,160},{224,1... | collective-permute-start | bytes 153608 | tf_op jit(solution)/shard_map/ppermute | solution.py:156
  15.3 30.9 %collective-permute-start.4 = (bf16[160,160]{1,0:T(8,128)(2,1)S(1)}, bf16[160,160]{1,0:T(8,128)(2,1)S(1)}, u32[]{:S(2)}, u32[]{:S(2)}) collective-permute-start(bf16[160,160]{1,0:T(8,128)(2,1)S(1)} %copy-done.4), channel_id=1, source_target_pairs={{0,64},{32,96},{64,0},{96,32},{128,192},{160,224},{192,128},{224,1... | collective-permute-start | bytes 153608 | tf_op jit(solution)/shard_map/ppermute | solution.py:156
  19.8 26.5 %collective-permute-start.5 = (bf16[160,160]{1,0:T(8,128)(2,1)S(1)}, bf16[160,160]{1,0:T(8,128)(2,1)S(1)}, u32[]{:S(2)}, u32[]{:S(2)}) collective-permute-start(bf16[160,160]{1,0:T(8,128)(2,1)S(1)} %copy-done.4), channel_id=1, source_target_pairs={{0,32},{32,0},{64,96},{96,64},{128,160},{160,128},{192,224},{224,1... | collective-permute-start | bytes 153608 | tf_op jit(solution)/shard_map/ppermute | solution.py:156
  47.5 7.5 %copy-start.1 = (bf16[16,32,1728]{2,1,0:T(8,128)(2,1)}, bf16[16,32,1728]{2,1,0:T(8,128)(2,1)S(1)}, u32[]{:S(2)}) copy-start(bf16[16,32,1728]{2,1,0:T(8,128)(2,1)S(1)} %all-to-all-done) | copy-start | bytes 5308420
  47.5 21.0 %all-to-all-start.1 = ((f32[32,8,640]{2,1,0:T(8,128)}), f32[32,8,640]{2,1,0:T(8,128)S(1)}, u32[]{:S(2)}, u32[]{:S(2)}) async-start(f32[32,8,640]{2,1,0:T(8,128)} %convolution_bitcast_fusion), calls=%async_computation.1 | async-start | bytes 1310720 | tf_op jit(solution)/shard_map/all_to_all | solution.py:165
  61.7 12.6 %collective-permute-start.1 = (bf16[8,32,512]{2,1,0:T(8,128)(2,1)}, bf16[8,32,512]{2,1,0:T(8,128)(2,1)S(1)}, u32[]{:S(2)}, u32[]{:S(2)}) collective-permute-start(bf16[8,32,512]{2,1,0:T(8,128)(2,1)} %get-tuple-element.9), channel_id=1, source_target_pairs={{0,32},{32,0},{64,96},{96,64},{128,160},{160,128},{192,224},{224,1... | collective-permute-start | bytes 786440 | tf_op jit(solution)/shard_map/ppermute | solution.py:171
  65.4 8.9 %collective-permute-start.2 = (bf16[8,32,352]{2,1,0:T(8,128)(2,1)}, bf16[8,32,352]{2,1,0:T(8,128)(2,1)S(1)}, u32[]{:S(2)}, u32[]{:S(2)}) collective-permute-start(bf16[8,32,352]{2,1,0:T(8,128)(2,1)} %get-tuple-element.10), channel_id=1, source_target_pairs={{0,480},{32,64},{64,32},{96,128},{128,96},{160,192},{192,160},{224... | collective-permute-start | bytes 540680 | tf_op jit(solution)/shard_map/ppermute | solution.py:172
  68.6 5.6 %copy-start.5 = (bf16[8,640]{1,0:T(8,128)(2,1)}, bf16[8,640]{1,0:T(8,128)(2,1)S(1)}, u32[]{:S(2)}) copy-start(bf16[8,640]{1,0:T(8,128)(2,1)S(1)} %reduce_sum.27.own_ref) | copy-start | bytes 30724
  68.6 5.6 %collective-permute-start.6 = (bf16[8,640]{1,0:T(8,128)(2,1)S(1)}, bf16[8,640]{1,0:T(8,128)(2,1)S(1)}, u32[]{:S(2)}, u32[]{:S(2)}) collective-permute-start(bf16[8,640]{1,0:T(8,128)(2,1)S(1)} %reduce_sum.27.own_ref), channel_id=1, source_target_pairs={{0,32},{32,0},{64,96},{96,64},{128,160},{160,128},{192,224},{224,1... | collective-permute-start | bytes 30728 | tf_op jit(solution)/shard_map/ppermute | solution.py:167
  74.2 0.6 copy-start.7
  74.3 0.7 copy-start.3
  74.3 0.8 copy-start.2
  119.7 1.9 %copy-start = (bf16[8,16,2432]{2,1,0:T(8,128)(2,1)}, bf16[8,16,2432]{2,1,0:T(8,128)(2,1)S(1)}, u32[]{:S(2)}) copy-start(bf16[8,16,2432]{2,1,0:T(8,128)(2,1)S(1)} %all_to_all.25.got_ref) | copy-start | bytes 1867780
  121.6 46.3 %all-to-all-start.3 = ((bf16[16,32,2560]{2,1,0:T(8,128)(2,1)}), bf16[16,32,2560]{2,1,0:T(8,128)(2,1)S(1)}, u32[]{:S(2)}, u32[]{:S(2)}) async-start(bf16[16,32,2560]{2,1,0:T(8,128)(2,1)} %broadcast_in_dim.15), calls=%async_computation.3 | async-start | bytes 5242880 | tf_op jit(solution)/shard_map/all_to_all | solution.py:22
  128.4 39.5 %collective-permute-start.7 = (bf16[432,2560]{1,0:T(8,128)(2,1)}, bf16[432,2560]{1,0:T(8,128)(2,1)}, u32[]{:S(2)}, u32[]{:S(2)}) collective-permute-start(bf16[432,2560]{1,0:T(8,128)(2,1)} %bitcast.33), channel_id=1, source_target_pairs={{0,1},{1,0},{2,3},{3,2},{4,5},{5,4},{6,7},{7,6},{8,9},{9,8},{10,11... | collective-permute-start | bytes 6635528 | tf_op jit(solution)/shard_map/ppermute | solution.py:152
